TPU v7x, 512 devices: a whole 4x8x8 slice. The times are simulated.
512 devices in a mesh: geo: 128 (over y, z, core), deg: 4 (over x).
Axes of the slice: x: 4, y: 8, z: 8, core: 2. Of those that a mesh axis runs over, the one named last changes fastest.
Arguments:
- lo_ainv: bfloat16 [20, 20, 65536], P(None, None, ('geo', 'deg')), may hold values from -1.25 to 1.25
- lo_geom: float32 [12, 65536], P(None, ('geo', 'deg')), may hold values from -1.5 to 1.5
- lo_load: bfloat16 [20, 65536], P(None, ('geo', 'deg')), may hold values from -6 to 6
- lo_degree: int32 [65536], P(('geo', 'deg')), may hold values from 1 to 3, as said below
- lo_send: int32 [4, 65536], P(None, ('geo', 'deg')), may hold values from 0 to 767, as said below
- hi_geom: float32 [12, 65536], P(None, ('geo', 'deg')), may hold values from -1.5 to 1.5
- hi_load: bfloat16 [84, 65536], P(None, ('geo', 'deg')), may hold values from -6 to 6
- hi_degree: int32 [65536], P(('geo', 'deg')), may hold values from 0 to 6, as said below
- hi_slot: int32 [65536], P(('geo', 'deg')), may hold values from -1 to 127, as said below
- hi_ainv: bfloat16 [84, 84, 65536], P(None, None, ('geo', 'deg')), may hold values from -0.625 to 0.625
- hi_send: int32 [4, 65536], P(None, ('geo', 'deg')), may hold values from -1 to 767, as said below
- recv_face: int32 [786432], P(('geo', 'deg')), may hold values from -1 to 767, as said below
- lift_ref: float32 [4, 4, 28, 84], replicated, may hold values from -1.25 to 1.25
- trace_ref: float32 [4, 84, 4, 28], replicated, may hold values from -1.25 to 1.25
- face_mass: float32 [28, 28], replicated, may hold values from -2 to 2
Outputs:
- low_particular: float32 [20, 65536], P(None, ('geo', 'deg'))
- high_particular: float32 [84, 65536], P(None, ('geo', 'deg'))
- trace_blocks: float32 [28, 28, 393216], P(None, None, ('geo', 'deg'))
- trace_rhs: float32 [28, 393216], P(None, ('geo', 'deg'))
Inputs may be any that keep to these rules, and one draw needn't show every extreme that they name: `lo_degree`: every LOW position holds an element of degree 1, 2 or 3. `hi_degree`: 0 where the position holds no element, else 4, 5 or 6. `hi_slot`: -1 exactly where hi_degree is 0; the other values are distinct on a device, so at most 32 elements go from one device to one device of its deg group; in some geo index every batch slot is filled. `lo_send`: values are distinct on a device, so at most 6 rows go from one device to one owner; some owners receive 6 LOW rows from every device of their deg index. `hi_send`: -1 exactly for the faces of batch slots that receive no element; the other values are distinct on a device; some owners receive 6 HIGH rows from every device of their deg index. `recv_face`: -1 exactly where no row arrives; a face of a device is named at most twice among that device's entries.
All inputs are finite; a program needn't handle non-finite values.
Results may differ from a plain program's by a relative error of at most 0.0095.
Values may be sent and summed in bfloat16 or wider, within the bound.
A program may use at most 64 MiB of HBM per device.

v0:
```python
import jax
import jax.numpy as jnp
from jax import lax
from jax.sharding import PartitionSpec as P

NI_LO = 20
NF_LO = 10


def prefix_masks(degree_value, inner_width, face_width):
    inner_count = (degree_value + 1.0) * (degree_value + 2.0) * (degree_value + 3.0) / 6.0
    face_count = (degree_value + 1.0) * (degree_value + 2.0) / 2.0
    inner_mask = (
        jnp.arange(inner_width, dtype=jnp.float32)[:, None] < inner_count[None, :]
    ).astype(jnp.float32)
    face_mask = (jnp.arange(face_width, dtype=jnp.float32)[:, None] < face_count[None, :]).astype(
        jnp.float32
    )
    return (inner_mask, face_mask)


def condense(inverse, geometry, load_values, degree_value, lift_table, trace_table, mass_table):
    term_count = lift_table.shape[0]
    face_width = mass_table.shape[0]
    element_count = geometry.shape[1]
    inner_mask, face_mask = prefix_masks(degree_value, inverse.shape[0], face_width)
    lift_mix = jnp.einsum(
        "kaij,ke->aije", lift_table, geometry[:term_count], precision=lax.Precision.HIGHEST
    )
    lift_mat = (lift_mix * face_mask[None, :, None, :] * inner_mask[None, None, :, :]).astype(
        jnp.bfloat16
    )
    trace_mix = jnp.einsum(
        "kjai,ke->jaie",
        trace_table,
        geometry[term_count : 2 * term_count],
        precision=lax.Precision.HIGHEST,
    )
    trace_mat = (trace_mix * inner_mask[:, None, None, :] * face_mask[None, None, :, :]).astype(
        jnp.bfloat16
    )
    solved = jnp.einsum(
        "jle,laie->jaie", inverse, trace_mat, preferred_element_type=jnp.float32
    ).astype(jnp.bfloat16)
    coupling = jnp.einsum("aije,jame->imae", lift_mat, solved, preferred_element_type=jnp.float32)
    scaling = geometry[2 * term_count : 2 * term_count + 4]
    pair_mask = face_mask[:, None, :] * face_mask[None, :, :]
    schur_block = (
        mass_table[:, :, None, None] * scaling[None, None, :, :] * pair_mask[:, :, None, :]
        - coupling
    )
    masked_load = load_values * inner_mask.astype(jnp.bfloat16)
    particular = inner_mask * jnp.einsum(
        "jle,le->je", inverse, masked_load, preferred_element_type=jnp.float32
    )
    rhs_part = -jnp.einsum(
        "aije,je->iae",
        lift_mat,
        particular.astype(jnp.bfloat16),
        preferred_element_type=jnp.float32,
    )
    face_rows = jnp.concatenate(
        [
            schur_block.reshape(face_width * face_width, 4 * element_count),
            rhs_part.reshape(face_width, 4 * element_count),
        ],
        axis=0,
    )
    return (face_rows.astype(jnp.bfloat16), particular)


def fill_buffer(face_rows, positions, slot_total):
    target = jnp.where(positions < 0, slot_total, positions)
    empty_buffer = jnp.zeros((face_rows.shape[0], slot_total), face_rows.dtype)
    return empty_buffer.at[:, target].set(face_rows, mode="drop")


def embed_rows(face_rows, narrow, wide_face):
    row_count = face_rows.shape[1]
    block_part = face_rows[: narrow * narrow].reshape(narrow, narrow, row_count)
    block_part = jnp.pad(block_part, ((0, wide_face - narrow), (0, wide_face - narrow), (0, 0)))
    right_part = jnp.pad(face_rows[narrow * narrow :], ((0, wide_face - narrow), (0, 0)))
    return jnp.concatenate(
        [block_part.reshape(wide_face * wide_face, row_count), right_part], axis=0
    )


def accumulate(blocks, right_side, arrived_rows, receive_plan, narrow):
    face_total = blocks.shape[2]
    block_width = min(512, face_total)
    pieces = []
    begin = 0
    while begin < face_total:
        width_here = min(block_width, face_total - begin)
        columns = begin + jnp.arange(width_here, dtype=jnp.int32)
        selector = (receive_plan[:, None] == columns[None, :]).astype(jnp.bfloat16)
        pieces.append(jnp.dot(arrived_rows, selector, preferred_element_type=jnp.float32))
        begin = begin + width_here
    summed = jnp.concatenate(pieces, axis=1)
    block_part = summed[: narrow * narrow].reshape(narrow, narrow, face_total)
    blocks = blocks.at[:narrow, :narrow].add(block_part)
    right_side = right_side.at[:narrow].add(summed[narrow * narrow :])
    return (blocks, right_side)


def on_device(
    lo_ainv,
    lo_geom,
    lo_load,
    lo_degree,
    lo_send,
    hi_geom,
    hi_load,
    hi_degree,
    hi_slot,
    hi_ainv,
    hi_send,
    recv_face,
    lift_ref,
    trace_ref,
    face_mass,
):
    wide_face = face_mass.shape[0]
    inner_width = hi_ainv.shape[0]
    geo_rows = hi_geom.shape[0]
    low_rows, low_particular = condense(
        lo_ainv,
        lo_geom,
        lo_load,
        lo_degree.astype(jnp.float32),
        lift_ref[:, :, :NF_LO, :NI_LO],
        trace_ref[:, :NI_LO, :, :NF_LO],
        face_mass[:NF_LO, :NF_LO],
    )
    record = jnp.concatenate(
        [hi_geom, hi_load.astype(jnp.float32), hi_degree.astype(jnp.float32)[None, :]], axis=0
    )
    outgoing = fill_buffer(record, hi_slot, hi_slot.shape[0])
    arrived = lax.all_to_all(outgoing, "deg", split_axis=1, concat_axis=1, tiled=True)
    high_rows, high_particular = condense(
        hi_ainv,
        arrived[:geo_rows],
        arrived[geo_rows : geo_rows + inner_width].astype(jnp.bfloat16),
        arrived[geo_rows + inner_width],
        lift_ref,
        trace_ref,
        face_mass,
    )
    groups = lax.axis_size("geo")
    cap_low = max(2, 6 * lo_ainv.shape[2] // groups)
    cap_high = max(2, 6 * hi_ainv.shape[2] // groups)
    per_owner = cap_low + cap_high
    face_total = (groups * per_owner + 1) // 2
    blocks = jnp.zeros((wide_face, wide_face, face_total), jnp.float32)
    right_side = jnp.zeros((wide_face, face_total), jnp.float32)
    low_positions = lo_send.reshape(-1)
    high_positions = hi_send.reshape(-1)
    low_target = jnp.where(
        low_positions < 0, -1, low_positions // cap_low * per_owner + low_positions % cap_low
    )
    high_target = jnp.where(
        high_positions < 0,
        -1,
        high_positions // cap_high * per_owner + cap_low + high_positions % cap_high,
    )
    combined = jnp.concatenate([embed_rows(low_rows, NF_LO, wide_face), high_rows], axis=1)
    positions = jnp.concatenate([low_target, high_target])
    arrived_rows = lax.all_to_all(
        fill_buffer(combined, positions, groups * per_owner),
        "geo",
        split_axis=1,
        concat_axis=1,
        tiled=True,
    )
    blocks, right_side = accumulate(blocks, right_side, arrived_rows, recv_face, wide_face)
    return (low_particular, high_particular, blocks, right_side)


def solution(mesh):
    in_specs = (
        P(None, None, ("geo", "deg")),
        P(None, ("geo", "deg")),
        P(None, ("geo", "deg")),
        P(("geo", "deg")),
        P(None, ("geo", "deg")),
        P(None, ("geo", "deg")),
        P(None, ("geo", "deg")),
        P(("geo", "deg")),
        P(("geo", "deg")),
        P(None, None, ("geo", "deg")),
        P(None, ("geo", "deg")),
        P(("geo", "deg")),
        P(),
        P(),
        P(),
    )
    out_specs = (
        P(None, ("geo", "deg")),
        P(None, ("geo", "deg")),
        P(None, None, ("geo", "deg")),
        P(None, ("geo", "deg")),
    )
    return jax.shard_map(
        on_device, mesh=mesh, in_specs=in_specs, out_specs=out_specs, check_vma=False
    )
```

profile of v0, /device:TPU:1, one launch (start us, length us, event | category | flops | bytes accessed | tf_op | source)
XLA Modules:
  0.0 217.8 jit_solution(9106446782423416625)
XLA Ops:
  5.0 4.8 %all-to-all-start = ((f32[97,4,32]{0,2,1:T(8,128)}), f32[97,4,32]{0,2,1:T(8,128)S(1)}, u32[]{:S(2)}, u32[]{:S(2)}) async-start(f32[97,4,32]{0,2,1:T(8,128)} %bitcast.9), calls=%async_computation | async-start | bytes 131072 | tf_op jit(solution)/shard_map/all_to_all | solution.py:139
  11.2 2.2 copy.112
  16.1 1.7 multiply_reduce_fusion.1
  17.8 1.7 copy.114
  21.9 2.7 %copy.111 = bf16[20,4,10,128]{0,2,3,1:T(8,128)(2,1)} copy(bf16[20,4,10,128]{3,2,1,0:T(8,128)(2,1)S(1)} %fusion.35) | data formatting | bytes 409600 | tf_op jit(solution)/shard_map/convert_element_type | solution.py:39
  25.1 4.3 %fusion.7 = bf16[10,10,4,128]{0,1,3,2:T(8,128)(2,1)} fusion(bf16[4,10,20,128]{2,1,3,0:T(8,128)(2,1)S(1)} %copy.114, bf16[20,4,10,128]{0,2,3,1:T(8,128)(2,1)} %copy.111, f32[10,10,128]{0,1,2:T(8,128)S(1)} %broadcast_multiply_fusion.1, f32[4,128]{1,0:T(4,128)S(1)} %slice-done, f32[10,10]{0,1:T(8,128)S(1)} %copy.107, bf16[20,20,128]{1,0,2:T(8,128)(2,1)} %copy.112), kind=kOutput, calls=%fused_computation.14 | convolution fusion | flops 6451200 | bytes 668048 | tf_op jit(solution)/shard_map/aije,jame->imae/dot_general | solution.py:45
  30.1 3.7 %copy.124 = bf16[84,84,128]{1,0,2:T(8,128)(2,1)S(1)} copy(bf16[84,84,128]{2,1,0:T(8,128)(2,1)} %param.32) | data formatting | bytes 3612672 | tf_op args[9]
  33.8 2.8 %copy.115 = bf16[10,10,512]{2,1,0:T(8,128)(2,1)S(1)} copy(bf16[10,10,512]{0,1,2:T(8,128)(2,1)} %bitcast.161) | data formatting | bytes 204800 | tf_op jit(solution)/shard_map/reshape | solution.py:80
  37.6 2.2 reshape.456
  43.2 10.3 %multiply_reduce_fusion = (f32[128,4,28]{0,2,1:T(8,128)S(1)}, bf16[4,28,84,128]{3,2,1,0:T(8,128)(2,1)}) fusion(f32[128,84]{0,1:T(8,128)} %copy.170, f32[84,128]{1,0:T(8,128)S(1)} %copy.122, f32[28,128]{1,0:T(8,128)S(1)} %fusion.50, f32[4,128,1,1]{0,1,3,2:T(8,128)S(1)} %bitcast.173, f32[4,4,28,84]{3,1,2,0:T(4,128)S(1)} %copy-done.1), kind=kOutput, calls=%fused_computation.10 | convolution fusion | flops 65013760 | bytes 2718720 | tf_op jit(solution)/shard_map/kaij,ke->aije/dot_general | solution.py:27
  53.5 7.7 %copy.128 = bf16[4,28,84,128]{2,1,3,0:T(8,128)(2,1)} copy(bf16[4,28,84,128]{3,2,1,0:T(8,128)(2,1)} %get-tuple-element.74) | data formatting | bytes 4816896 | tf_op jit(solution)/shard_map/convert_element_type | solution.py:30
  61.2 9.3 %fusion.4 = bf16[84,4,28,128]{3,0,2,1:T(8,128)(2,1)} fusion(f32[28,128]{1,0:T(8,128)S(1)} %fusion.50, f32[84,128]{1,0:T(8,128)S(1)} %copy.122, f32[4,128,1,1]{0,1,3,2:T(8,128)S(1)} %bitcast.172, f32[4,84,4,28]{1,2,3,0:T(4,128)S(1)} %copy-done.3), kind=kOutput, calls=%fused_computation.9 | convolution fusion | flops 61415424 | bytes 2618368 | tf_op jit(solution)/shard_map/kjai,ke->jaie/dot_general | solution.py:33
  70.5 7.7 %copy.123 = bf16[84,4,28,128]{0,2,3,1:T(8,128)(2,1)} copy(bf16[84,4,28,128]{3,0,2,1:T(8,128)(2,1)} %fusion.4) | data formatting | bytes 4816896 | tf_op jit(solution)/shard_map/convert_element_type | solution.py:39
  78.2 1.9 broadcast_multiply_fusion
  80.2 8.0 %fusion = bf16[28,28,4,128]{0,1,3,2:T(8,128)(2,1)} fusion(f32[28,28,128]{0,1,2:T(8,128)} %broadcast_multiply_fusion, f32[4,128]{1,0:T(4,128)S(1)} %copy.117, f32[28,28]{0,1:T(8,128)S(1)} %copy.116, bf16[4,28,84,128]{2,1,3,0:T(8,128)(2,1)} %copy.128, bf16[84,4,28,128]{0,2,3,1:T(8,128)(2,1)} %copy.123, bf16[84,84,128]{1,0,2:T(8,128)(2,1)S(1)} %copy.124), kind=kOutput, calls=%fused_computation.3 | convolution fusion | flops 272556032 | bytes 7832640 | tf_op jit(solution)/shard_map/aije,jame->imae/dot_general | solution.py:45
  88.2 5.6 %copy.129 = bf16[28,28,4,128]{3,2,1,0:T(4,128)(2,1)S(1)} copy(bf16[28,28,4,128]{0,1,3,2:T(8,128)(2,1)} %fusion) | data formatting | bytes 1605632 | tf_op jit(solution)/shard_map/convert.4
  94.2 2.4 %copy.130 = bf16[1024,812]{1,0:T(8,128)(2,1)} copy(bf16[1024,812]{0,1:T(8,128)(2,1)S(1)} %fusion.28) | data formatting | bytes 3325952 | tf_op jit(solution)/shard_map/concatenate | solution.py:166
  96.7 6.8 %scatter_custom_fusion.1 = bf16[812,1536]{0,1:T(8,128)(2,1)S(1)} fusion(s32[1024]{0:T(1024)} %bitcast.177, bf16[1024,812]{1,0:T(8,128)(2,1)} %copy.130, bf16[]{:T(256)} %constant.124.clone.1), kind=kCustom, calls=%fused_computation.37 | custom fusion | bytes 2494976 | tf_op jit(solution)/shard_map/scatter | solution.py:75
  103.4 2.6 %all_to_all.16 = bf16[812,128,12]{0,2,1:T(8,128)(2,1)} reshape(bf16[812,1536]{0,1:T(8,128)(2,1)S(1)} %scatter_custom_fusion.1) | data formatting | bytes 4988928 | tf_op jit(solution)/shard_map/all_to_all | solution.py:168
  106.1 18.3 %all-to-all-start.1 = ((bf16[812,128,12]{0,2,1:T(8,128)(2,1)}), bf16[812,128,12]{0,2,1:T(8,128)(2,1)}, u32[]{:S(2)}, u32[]{:S(2)}) async-start(bf16[812,128,12]{0,2,1:T(8,128)(2,1)} %all_to_all.16), calls=%async_computation.1 | async-start | bytes 7340032 | tf_op jit(solution)/shard_map/all_to_all | solution.py:168
  125.1 83.1 %all-to-all-done.1 = bf16[812,128,12]{0,2,1:T(8,128)(2,1)} async-done(((bf16[812,128,12]{0,2,1:T(8,128)(2,1)}), bf16[812,128,12]{0,2,1:T(8,128)(2,1)}, u32[]{:S(2)}, u32[]{:S(2)}) %all-to-all-start.1) | async-done | bytes 2494496 | tf_op jit(solution)/shard_map/all_to_all | solution.py:168
  208.2 4.3 %all_to_all.18 = bf16[812,1536]{0,1:T(8,128)(2,1)S(1)} reshape(bf16[812,128,12]{0,2,1:T(8,128)(2,1)} %all-to-all-done.1) | data formatting | bytes 4988928 | tf_op jit(solution)/shard_map/all_to_all | solution.py:168
  212.5 1.6 fusion.14
  216.1 1.7 add.188
  (75 shorter events, 19.5 us)
Async XLA Ops:
  0.6 20.0 %copy-start.4 = (f32[12,128]{1,0:T(8,128)S(1)}, f32[12,128]{1,0:T(8,128)}, u32[]{:S(2)}) copy-start(f32[12,128]{1,0:T(8,128)} %param.24) | copy-start | bytes 18436
  5.0 34.8 %all-to-all-start = ((f32[97,4,32]{0,2,1:T(8,128)}), f32[97,4,32]{0,2,1:T(8,128)S(1)}, u32[]{:S(2)}, u32[]{:S(2)}) async-start(f32[97,4,32]{0,2,1:T(8,128)} %bitcast.9), calls=%async_computation | async-start | bytes 131072 | tf_op jit(solution)/shard_map/all_to_all | solution.py:139
  19.4 5.5 %copy-start.2 = (f32[28,28]{1,0:T(8,128)S(1)}, f32[28,28]{1,0:T(8,128)}, u32[]{:S(2)}) copy-start(f32[28,28]{1,0:T(8,128)} %param.37) | copy-start | bytes 9412
  19.5 5.6 %copy-start.5 = (s32[4,128]{1,0:T(4,128)S(1)}, s32[4,128]{1,0:T(4,128)}, u32[]{:S(2)}) copy-start(s32[4,128]{1,0:T(4,128)} %param.27) | copy-start | bytes 6148
  19.5 5.6 %copy-start.6 = (s32[4,128]{1,0:T(4,128)S(1)}, s32[4,128]{1,0:T(4,128)}, u32[]{:S(2)}) copy-start(s32[4,128]{1,0:T(4,128)} %param.33) | copy-start | bytes 6148
  19.5 5.6 %slice-start = ((f32[12,128]{1,0:T(8,128)}), f32[4,128]{1,0:T(4,128)S(1)}, s32[]{:S(2)}) async-start(f32[12,128]{1,0:T(8,128)} %param.24), calls=%async_computation.2 | async-start | bytes 4096 | tf_op jit(solution)/shard_map/slice | solution.py:46
  37.6 5.6 %copy-start.1 = (f32[4,4,28,84]{3,1,2,0:T(4,128)S(1)}, f32[4,4,28,84]{3,1,2,0:T(4,128)}, u32[]{:S(2)}) copy-start(f32[4,4,28,84]{3,1,2,0:T(4,128)} %param.35) | copy-start | bytes 451588
  53.5 7.7 %copy-start.3 = (f32[4,84,4,28]{1,2,3,0:T(4,128)S(1)}, f32[4,84,4,28]{1,2,3,0:T(4,128)}, u32[]{:S(2)}) copy-start(f32[4,84,4,28]{1,2,3,0:T(4,128)} %param.36) | copy-start | bytes 451588
  88.2 5.8 %copy-start = (bf16[784,512]{1,0:T(8,128)(2,1)S(1)}, bf16[784,512]{1,0:T(8,128)(2,1)}, u32[]{:S(2)}) copy-start(bf16[784,512]{1,0:T(8,128)(2,1)} %reshape.456) | copy-start | bytes 2408452
  106.1 102.1 %all-to-all-start.1 = ((bf16[812,128,12]{0,2,1:T(8,128)(2,1)}), bf16[812,128,12]{0,2,1:T(8,128)(2,1)}, u32[]{:S(2)}, u32[]{:S(2)}) async-start(bf16[812,128,12]{0,2,1:T(8,128)(2,1)} %all_to_all.16), calls=%async_computation.1 | async-start | bytes 7340032 | tf_op jit(solution)/shard_map/all_to_all | solution.py:168
  125.1 87.4 %copy-start.7 = (s32[1536]{0:T(1024)S(1)}, s32[1536]{0:T(1024)}, u32[]{:S(2)}) copy-start(s32[1536]{0:T(1024)} %param.34) | copy-start | bytes 18436
where the time goes:
time: 222 us; the launch traced here: 218 us
  waiting for transfers between devices  83.1 us (37%)
  local copies, waits for them, and re-layouts  61.4 us (28%)
  matrix products  39.2 us (18%)
  starting transfers between devices  23.1 us (10%)
  other arithmetic  9.99 us (4%)
    all_to_all x1, waiting for transfers between devices, on_device(): lax.all_to_all(fill_buffer(combined, positions, groups * per_owner), 'geo...  83.1 us
    all_to_all x1, starting transfers between devices, on_device(): lax.all_to_all(fill_buffer(combined, positions, groups * per_owner), 'geo...  18.3 us
    dot_general x2, matrix products, condense(): jnp.einsum('aije,jame->imae', lift_mat, solved, preferred_element_type=jn...  12.3 us
    dot_general x2, matrix products, condense(): jnp.einsum('kaij,ke->aije', lift_table, geometry[:term_count], precision=...  12 us
    dot_general x2, matrix products, condense(): jnp.einsum('kjai,ke->jaie', trace_table, geometry[term_count:2 * term_cou...  10.5 us
    convert_element_type x2, local copies, waits for them, and re-layouts, condense(): (trace_mix * inner_mask[:, None, None, :] * face_mask[None, None, :, :])....  10.4 us
    convert_element_type x2, local copies, waits for them, and re-layouts, condense(): (lift_mix * face_mask[None, :, None, :] * inner_mask[None, None, :, :]).a...  9.37 us
    unnamed x31, local copies, waits for them, and re-layouts  8.98 us
  transfers between devices with their start and end apart: 2, of which 1 were waited for; matrix products, arithmetic and copies ran while one was open for 14% of the time, Pallas kernels for 0%

commit v1 on v0

v1 whole, which is shorter than its diff:
```python
import functools

import jax
import jax.numpy as jnp
from jax import lax
from jax.experimental import pallas as pl
from jax.experimental.pallas import tpu as pltpu
from jax.sharding import PartitionSpec as P

F32 = jnp.float32
BF16 = jnp.bfloat16
LANES = 128
TERMS = 4
NF_LO = 10
NI_LO = 20
LO_PAD = 16
LO_STRIDE = 12
HI_PAD = 32
HI_STRIDE = 32
NT = (((1,), (1,)), ((), ()))
TN = (((0,), (0,)), ((), ()))
VMEM = pl.BlockSpec(memory_space=pltpu.VMEM)


def masks(degree, inner_width, face_width):
    inner_count = (degree + 1.0) * (degree + 2.0) * (degree + 3.0) / 6.0
    face_count = (degree + 1.0) * (degree + 2.0) / 2.0
    elements = degree.shape[1]
    inner_row = lax.broadcasted_iota(jnp.int32, (inner_width, elements), 0).astype(F32)
    face_row = lax.broadcasted_iota(jnp.int32, (face_width, elements), 0).astype(F32)
    inner_mask = (inner_row < inner_count).astype(F32)
    face_mask = (face_row < face_count).astype(F32)
    return inner_mask, face_mask


def condense_body(
    ainv_ref, geom, load, degree, lift_ref, trace_ref, mass_ref, part_ref,
    lmat, solved, masked, rhs_load, stack, massb, width, inner, pad, stride, rows
):
    am = 4 * width
    inner_mask, face_mask = masks(degree, inner, pad)
    masked[...] = inner_mask
    rhs_load[...] = load * inner_mask
    for t in range(TERMS):
        for a in range(4):
            piece = lift_ref[t, a][:width, :inner]
            piece = jnp.concatenate([piece, jnp.zeros((pad - width, inner), F32)], axis=0)
            lmat[a, t * pad:(t + 1) * pad, :] = piece.astype(BF16)
    mass = mass_ref[...][:width, :width]
    mass = jnp.concatenate([mass, jnp.zeros((pad - width, width), F32)], axis=0)
    for m in range(width):
        massb[m] = jnp.broadcast_to(mass[:, m:m + 1], (pad, LANES))
    trace_g = [geom[TERMS + t:TERMS + t + 1, :] for t in range(TERMS)]

    def solve(pair, carry):
        blocks = []
        rows_mask = []
        for k in range(2):
            j = 2 * pair + k
            block = ainv_ref[j].astype(F32)
            row_mask = masked[pl.ds(j, 1), :]
            part_ref[pl.ds(j, 1), :] = row_mask * jnp.sum(block * rhs_load[...], axis=0, keepdims=True)
            blocks.append((block * masked[...]).astype(BF16))
            rows_mask.append(row_mask)
        out = jnp.dot(trace_ref[...], jnp.concatenate(blocks, axis=1), preferred_element_type=F32)
        for k in range(2):
            j = 2 * pair + k
            total = None
            for t in range(TERMS):
                term = out[t * am:(t + 1) * am, k * LANES:(k + 1) * LANES] * (trace_g[t] * rows_mask[k])
                total = term if total is None else total + term
            solved[pl.ds(pl.multiple_of(j * am, 8), am), :] = total
        return carry

    lax.fori_loop(0, inner // 2, solve, 0)

    lift_g = [geom[t:t + 1, :] for t in range(TERMS)]

    def mixed(out, k):
        total = None
        for t in range(TERMS):
            term = out[t * pad:(t + 1) * pad, k * LANES:(k + 1) * LANES] * lift_g[t]
            total = term if total is None else total + term
        return total

    part = part_ref[...].astype(BF16)
    for a in range(4):
        out = jnp.dot(lmat[a], part, preferred_element_type=F32)
        value = -(mixed(out, 0) * face_mask)
        stack[pl.ds(a * rows + width, width, stride=stride), :] = value[:width]
    scales = [geom[2 * TERMS + a:2 * TERMS + a + 1, :] for a in range(4)]

    def couple(pair, carry):
        for a in range(4):
            columns = []
            for k in range(2):
                m = 2 * pair + k
                columns.append(solved[pl.ds(a * width + m, inner, stride=am), :].astype(BF16))
            out = jnp.dot(lmat[a], jnp.concatenate(columns, axis=1), preferred_element_type=F32)
            for k in range(2):
                m = 2 * pair + k
                column_mask = (m.astype(F32) < (degree + 1.0) * (degree + 2.0) / 2.0).astype(F32)
                value = (massb[m] * scales[a] - mixed(out, k)) * (face_mask * column_mask)
                stack[pl.ds(a * rows + m, width, stride=stride), :] = value[:width]
        return carry

    lax.fori_loop(0, width // 2, couple, 0)


def one_hots(send_ref, chosen, capacity):
    groups = chosen.shape[0] // capacity
    for a in range(4):
        positions = send_ref[a:a + 1, :]
        for c in range(capacity):
            want = lax.broadcasted_iota(jnp.int32, (groups, LANES), 0) * capacity + c
            chosen[c * groups:(c + 1) * groups, a * LANES:(a + 1) * LANES] = (
                (want == positions).astype(F32).astype(BF16)
            )


def record_kernel(geom_ref, load_ref, degree_ref, slot_ref, out_ref):
    count = geom_ref.shape[0] + load_ref.shape[0] + 1
    record = jnp.concatenate(
        [load_ref[...].astype(F32), geom_ref[...], degree_ref[...].astype(F32),
         jnp.zeros((LANES - count, LANES), F32)], axis=0
    )
    hot = (lax.broadcasted_iota(jnp.int32, (LANES, LANES), 0) == slot_ref[...]).astype(F32)
    out_ref[...] = lax.dot_general(hot, record, NT, precision=lax.Precision.HIGHEST, preferred_element_type=F32)


def low_kernel(
    capacity, ainv_ref, geom_ref, load_ref, degree_ref, send_ref, lift_ref, trace_ref, mass_ref,
    part_ref, placed_ref, lmat, solved, masked, rhs_load, stack, massb, chosen, rowsb
):
    stack[...] = jnp.zeros_like(stack)
    condense_body(
        ainv_ref, geom_ref[...], load_ref[...].astype(F32), degree_ref[...].astype(F32), lift_ref, trace_ref,
        mass_ref, part_ref, lmat, solved, masked, rhs_load, stack, massb,
        NF_LO, NI_LO, LO_PAD, LO_STRIDE, LANES,
    )
    one_hots(send_ref, chosen, capacity)
    for a in range(4):
        rowsb[:, a * LANES:(a + 1) * LANES] = stack[a * LANES:(a + 1) * LANES, :].astype(BF16)
    placed_ref[...] = lax.dot_general(chosen[...], rowsb[...], NT, preferred_element_type=F32)


def high_kernel(
    capacity, ainv_ref, record_ref, send_ref, lift_ref, trace_ref, mass_ref, low_ref,
    part_ref, out_ref, lmat, solved, masked, rhs_load, stack, massb, chosen, rowsb, rec, wide
):
    inner = ainv_ref.shape[0]
    width = mass_ref.shape[0]
    tiles = width * HI_STRIDE // LANES
    groups = out_ref.shape[0]
    per = out_ref.shape[1]
    rec[...] = record_ref[...].T
    geom = rec[inner:inner + 12, :]
    degree = rec[inner + 12:inner + 13, :]
    stack[...] = jnp.zeros_like(stack)
    condense_body(
        ainv_ref, geom, rec[:inner, :], degree, lift_ref, trace_ref, mass_ref, part_ref,
        lmat, solved, masked, rhs_load, stack, massb,
        width, inner, HI_PAD, HI_STRIDE, width * HI_STRIDE,
    )
    one_hots(send_ref, chosen, capacity)
    rows = width * HI_STRIDE
    for c in range(capacity):
        wide[pl.ds(c * (tiles + 1) + tiles, groups, stride=per), :] = low_ref[c * groups:(c + 1) * groups, :]

    def place(q, carry):
        for a in range(4):
            piece = stack[pl.ds(pl.multiple_of(a * rows + q * LANES, LANES), LANES), :]
            rowsb[:, a * LANES:(a + 1) * LANES] = piece.astype(BF16)
        got = lax.dot_general(chosen[...], rowsb[...], NT, preferred_element_type=F32)
        for c in range(capacity):
            wide[pl.ds(c * (tiles + 1) + q, groups, stride=per), :] = got[c * groups:(c + 1) * groups, :]
        return carry

    lax.fori_loop(0, tiles, place, 0)

    def narrow(o, carry):
        out_ref[o] = wide[pl.ds(pl.multiple_of(o * per, 8), per), :].astype(BF16)
        return carry

    lax.fori_loop(0, groups, narrow, 0)


def accumulate_kernel(capacity, rows_ref, recv_ref, blocks_ref, rhs_ref, wide, hot_lo, hot_hi, low_sum, rhs_sum):
    q = pl.program_id(0)
    groups, per, _ = rows_ref.shape
    faces = blocks_ref.shape[2]
    tiles = per // capacity - 1
    width = blocks_ref.shape[1]
    per_tile = LANES // HI_STRIDE

    def gathered(at):
        pieces = [
            wide[pl.ds(c * (tiles + 1) + at, groups, stride=per), :].astype(BF16) for c in range(capacity)
        ]
        return jnp.concatenate(pieces, axis=0)

    @pl.when(q == 0)
    def _():
        def widen(g, carry):
            wide[pl.ds(pl.multiple_of(g * per, 8), per), :] = rows_ref[g].astype(F32)
            return carry

        lax.fori_loop(0, groups, widen, 0)
        columns = lax.broadcasted_iota(jnp.int32, (groups, faces), 1)
        for c in range(capacity):
            hot_lo[c * groups:(c + 1) * groups, :] = (recv_ref[:, c:c + 1] == columns).astype(F32).astype(BF16)
            hot_hi[c * groups:(c + 1) * groups, :] = (
                (recv_ref[:, capacity + c:capacity + c + 1] == columns).astype(F32).astype(BF16)
            )
        low_sum[...] = lax.dot_general(gathered(tiles), hot_lo[...], TN, preferred_element_type=F32)

    total = lax.dot_general(gathered(q), hot_hi[...], TN, preferred_element_type=F32)
    for k in range(per_tile):
        blocks_ref[k] = total[k * HI_STRIDE:k * HI_STRIDE + width, :]
        rhs_ref[k] = total[k * HI_STRIDE + width:k * HI_STRIDE + width + 1, :]
    for s in range(-(-NF_LO // per_tile)):
        @pl.when(q == s)
        def _():
            for k in range(per_tile):
                i = s * per_tile + k
                if i < NF_LO:
                    low = low_sum[i * LO_STRIDE:i * LO_STRIDE + NF_LO + 1, :]
                    blocks_ref[k, :NF_LO, :] = blocks_ref[k, :NF_LO, :] + low[:NF_LO]
                    rhs_ref[k] = rhs_ref[k] + low[NF_LO:NF_LO + 1]


def on_device(
    lo_ainv, lo_geom, lo_load, lo_degree, lo_send, hi_geom, hi_load, hi_degree, hi_slot, hi_ainv, hi_send,
    recv_face, lift_ref, trace_ref, face_mass,
):
    width = face_mass.shape[0]
    inner, _, elements = hi_ainv.shape
    groups = lax.axis_size("geo")
    capacity = 6 * lo_ainv.shape[2] // groups
    tiles = width * HI_STRIDE // LANES
    per = capacity * (tiles + 1)
    rows = width * HI_STRIDE
    faces = groups * capacity

    record = pl.pallas_call(
        record_kernel,
        out_shape=jax.ShapeDtypeStruct((elements, LANES), F32),
        in_specs=[VMEM] * 4,
        out_specs=VMEM,
        name="record",
    )(hi_geom, hi_load, hi_degree[None, :], hi_slot[None, :])
    record = lax.all_to_all(record, "deg", split_axis=0, concat_axis=0, tiled=True)

    turned = jnp.transpose(trace_ref, (0, 2, 3, 1))
    trace_hi = turned.reshape(TERMS * 4 * width, inner).astype(BF16)
    trace_lo = turned[:, :, :NF_LO, :NI_LO].reshape(TERMS * 4 * NF_LO, NI_LO).astype(BF16)

    low_particular, placed = pl.pallas_call(
        functools.partial(low_kernel, capacity),
        out_shape=(
            jax.ShapeDtypeStruct((NI_LO, elements), F32),
            jax.ShapeDtypeStruct((groups * capacity, LANES), F32),
        ),
        in_specs=[VMEM] * 8,
        out_specs=(VMEM, VMEM),
        scratch_shapes=[
            pltpu.VMEM((4, TERMS * LO_PAD, NI_LO), BF16),
            pltpu.VMEM((NI_LO * 4 * NF_LO, LANES), F32),
            pltpu.VMEM((NI_LO, LANES), F32),
            pltpu.VMEM((NI_LO, LANES), F32),
            pltpu.VMEM((4 * LANES, LANES), F32),
            pltpu.VMEM((NF_LO, LO_PAD, LANES), F32),
            pltpu.VMEM((groups * capacity, 4 * LANES), BF16),
            pltpu.VMEM((LANES, 4 * LANES), BF16),
        ],
        cost_estimate=pl.CostEstimate(flops=400_000_000, bytes_accessed=2_000_000, transcendentals=0),
        name="low",
    )(lo_ainv, lo_geom, lo_load, lo_degree[None, :], lo_send, lift_ref, trace_lo, face_mass)

    high_particular, outgoing = pl.pallas_call(
        functools.partial(high_kernel, capacity),
        out_shape=(
            jax.ShapeDtypeStruct((inner, elements), F32),
            jax.ShapeDtypeStruct((groups, per, LANES), BF16),
        ),
        in_specs=[VMEM] * 7,
        out_specs=(VMEM, VMEM),
        scratch_shapes=[
            pltpu.VMEM((4, TERMS * HI_PAD, inner), BF16),
            pltpu.VMEM((inner * 4 * width, LANES), F32),
            pltpu.VMEM((inner, LANES), F32),
            pltpu.VMEM((inner, LANES), F32),
            pltpu.VMEM((4 * rows, LANES), F32),
            pltpu.VMEM((width, HI_PAD, LANES), F32),
            pltpu.VMEM((groups * capacity, 4 * LANES), BF16),
            pltpu.VMEM((LANES, 4 * LANES), BF16),
            pltpu.VMEM((LANES, LANES), F32),
            pltpu.VMEM((groups * per, LANES), F32),
        ],
        compiler_params=pltpu.CompilerParams(vmem_limit_bytes=48 << 20),
        name="high",
    )(hi_ainv, record, hi_send, lift_ref, trace_hi, face_mass, placed)

    arrived = lax.all_to_all(outgoing, "geo", split_axis=0, concat_axis=0, tiled=True)

    plan = recv_face.reshape(groups, 2 * capacity)
    per_tile = LANES // HI_STRIDE
    blocks, right = pl.pallas_call(
        functools.partial(accumulate_kernel, capacity),
        out_shape=(
            jax.ShapeDtypeStruct((width, width, faces), F32),
            jax.ShapeDtypeStruct((width, 1, faces), F32),
        ),
        grid=(tiles,),
        in_specs=[
            pl.BlockSpec((groups, per, LANES), lambda q: (0, 0, 0)),
            pl.BlockSpec((groups, 2 * capacity), lambda q: (0, 0)),
        ],
        out_specs=(
            pl.BlockSpec((per_tile, width, faces), lambda q: (q, 0, 0)),
            pl.BlockSpec((per_tile, 1, faces), lambda q: (q, 0, 0)),
        ),
        scratch_shapes=[
            pltpu.VMEM((groups * per, LANES), F32),
            pltpu.VMEM((groups * capacity, faces), BF16),
            pltpu.VMEM((groups * capacity, faces), BF16),
            pltpu.VMEM((LANES, faces), F32),
            pltpu.VMEM((8, LANES), F32),
        ],
        compiler_params=pltpu.CompilerParams(vmem_limit_bytes=48 << 20),
        name="accumulate",
    )(arrived, plan)
    return (low_particular, high_particular, blocks, right.reshape(width, faces))


def solution(mesh):
    both = ("geo", "deg")
    in_specs = (
        P(None, None, both), P(None, both), P(None, both), P(both), P(None, both), P(None, both), P(None, both),
        P(both), P(both), P(None, None, both), P(None, both), P(both), P(), P(), P(),
    )
    out_specs = (P(None, both), P(None, both), P(None, None, both), P(None, both))
    return jax.shard_map(on_device, mesh=mesh, in_specs=in_specs, out_specs=out_specs, check_vma=False)
```

time: 222 us -> 103 us (0.46); the launches traced: 218 us -> 102 us
  local copies, waits for them, and re-layouts: 61.4 us -> 5.12 us
  waiting for transfers between devices: 83.1 us -> 41 us
  matrix products: 39.2 us -> 0 us
  Pallas kernels: 0 us -> 31.8 us
  other arithmetic: 9.99 us -> 0.98 us
    all_to_all x2, waiting for transfers between devices: 83.1 us -> 41 us  [the longest x1 41 us: on_device(): lax.all_to_all(outgoing, 'geo', split_axis=0, concat_axis=0, tiled=True)]
    dot_general x9 -> x0, matrix products: 39.2 us -> none  [the longest x2 12.3 us: condense(): jnp.einsum('aije,jame->imae', lift_mat, solved, preferred_element_type=jn...]
    pallas_call x0 -> x4, Pallas kernels: none -> 31.8 us  [the longest x1 19.3 us: on_device(): pl.pallas_call(functools.partial(high_kernel, capacity), out_shape=(jax.S...]
    convert_element_type x7 -> x3, local copies, waits for them, and re-layouts: 20.1 us -> 0.7 us  [the longest x2 0.66 us: on_device(): turned[:, :, :NF_LO, :NI_LO].reshape(TERMS * 4 * NF_LO, NI_LO).astype(BF16)]
    scatter x2 -> x0, local copies, waits for them, and re-layouts: 8.22 us -> none  [fill_buffer(): return empty_buffer.at[:, target].set(face_rows, mode='drop')]
    all_to_all x2 -> x0, local copies, waits for them, and re-layouts: 6.91 us -> none  [on_device(): lax.all_to_all(fill_buffer(combined, positions, groups * per_owner), 'geo...]
    another operation x1, local copies, waits for them, and re-layouts: 5.57 us -> 0.02 us
    reshape x2 -> x1, local copies, waits for them, and re-layouts: 4.95 us -> 0.1 us  [on_device(): plan = recv_face.reshape(groups, 2 * capacity)]
  transfers between devices with their start and end apart: 2 -> 2, of which waited for: 1 -> 1; matrix products, arithmetic and copies ran while one was open for 14% -> 3% of each run, Pallas kernels for 0% -> 5%
where the time goes in v1:
time: 103 us; the launch traced here: 102 us
  waiting for transfers between devices  41 us (40%)
  Pallas kernels  31.8 us (31%)
  starting transfers between devices  22.9 us (22%)
  local copies, waits for them, and re-layouts  5.12 us (5%)
    all_to_all x1, waiting for transfers between devices, on_device(): lax.all_to_all(outgoing, 'geo', split_axis=0, concat_axis=0, tiled=True)  41 us
    pallas_call x1, Pallas kernels, on_device(): pl.pallas_call(functools.partial(high_kernel, capacity), out_shape=(jax.S...  19.3 us
    all_to_all x1, starting transfers between devices, on_device(): lax.all_to_all(outgoing, 'geo', split_axis=0, concat_axis=0, tiled=True)  18 us
    pallas_call x1, Pallas kernels, on_device(): pl.pallas_call(functools.partial(accumulate_kernel, capacity), out_shape=...  6.02 us
    all_to_all x1, starting transfers between devices, on_device(): lax.all_to_all(record, 'deg', split_axis=0, concat_axis=0, tiled=True)  4.84 us
    pallas_call x1, Pallas kernels, on_device(): pl.pallas_call(functools.partial(low_kernel, capacity), out_shape=(jax.Sh...  4.81 us
    unnamed x14, local copies, waits for them, and re-layouts  4.28 us
  transfers between devices with their start and end apart: 2, of which 1 were waited for; matrix products, arithmetic and copies ran while one was open for 3% of the time, Pallas kernels for 5%

profile of v1, /device:TPU:1, one launch (start us, length us, event | category | flops | bytes accessed | tf_op | source)
XLA Modules:
  0.0 102.5 jit_solution(5216094939724449652)
XLA Ops:
  0.6 0.0 copy-start.3
  0.6 0.0 copy-start.4
  0.7 0.0 copy-start
  0.7 1.7 %record.1 = f32[128,128]{1,0:T(8,128)} custom-call(f32[12,128]{1,0:T(8,128)} %geom_ref.3, bf16[84,128]{1,0:T(8,128)(2,1)} %load_ref.3, s32[1,128]{1,0:T(1,128)} %bitcast.13, s32[1,128]{1,0:T(1,128)} %bitcast.14), custom_call_target="tpu_custom_call" | custom-call | tf_op jit(solution)/shard_map/record/pallas_call | solution.py:245
  2.4 4.8 %all-to-all-start = ((f32[4,32,128]{2,1,0:T(8,128)}), f32[4,32,128]{2,1,0:T(8,128)S(1)}, u32[]{:S(2)}, u32[]{:S(2)}) async-start(f32[4,32,128]{2,1,0:T(8,128)} %bitcast.11), calls=%async_computation | async-start | bytes 131072 | tf_op jit(solution)/shard_map/all_to_all | solution.py:252
  7.2 1.0 convert_bitcast_fusion
  8.3 0.6 reshape.22.trace_ref
  9.0 1.7 %copy.24.lift_ref = f32[4,4,28,84]{3,2,1,0:T(8,128)} copy(f32[4,4,28,84]{3,1,2,0:T(4,128)} %param.27) | data formatting | bytes 301056 | tf_op args[12]
  10.7 4.8 %low.1 = (f32[20,128]{1,0:T(8,128)}, f32[768,128]{1,0:T(8,128)}) custom-call(bf16[20,20,128]{2,1,0:T(8,128)(2,1)} %ainv_ref.2, f32[12,128]{1,0:T(8,128)} %geom_ref.2, bf16[20,128]{1,0:T(8,128)(2,1)} %load_ref.2, s32[1,128]{1,0:T(1,128)} %bitcast.15, s32[4,128]{1,0:T(4,128)} %send_ref.2, f32[4,4,28,84]{3,2,1,0:T(8,128)} %copy.24.lift_ref, ...), custom_call_target="tpu_custom_call" | custom-call | flops 400000000 | bytes 2000000 | tf_op jit(solution)/shard_map/low/pallas_call | solution.py:258
  15.5 0.0 all-to-all-done
  15.5 0.0 copy-done.3
  15.5 0.0 copy-done.4
  15.5 0.0 copy-done
  15.5 0.0 copy-start.1
  15.5 0.9 copy-done.1
  16.5 0.0 copy-start.2
  16.5 1.0 copy-done.2
  17.5 19.3 %high.1 = (f32[84,128]{1,0:T(8,128)}, bf16[128,48,128]{2,1,0:T(8,128)(2,1)}) custom-call(bf16[84,84,128]{2,1,0:T(8,128)(2,1)S(1)} %copy-done, f32[128,128]{1,0:T(8,128)S(1)} %bitcast.10, s32[4,128]{1,0:T(4,128)S(1)} %copy-done.4, f32[4,4,28,84]{3,2,1,0:T(8,128)S(1)} %copy-done.1, bf16[448,84]{1,0:T(8,128)(2,1)S(1)} %convert_element_type.7.trace_ref, ...), custom_call_target="tpu_custom_call" | custom-call | tf_op jit(solution)/shard_map/high/pallas_call | solution.py:280
  36.7 18.0 %all-to-all-start.1 = ((bf16[128,48,128]{2,1,0:T(8,128)(2,1)}), bf16[128,48,128]{2,1,0:T(8,128)(2,1)S(1)}, u32[]{:S(2)}, u32[]{:S(2)}) async-start(bf16[128,48,128]{2,1,0:T(8,128)(2,1)} %get-tuple-element.13), calls=%async_computation.1 | async-start | bytes 3145728 | tf_op jit(solution)/shard_map/all_to_all | solution.py:304
  54.7 0.0 copy-done.5
  54.7 0.1 reshape.20.recv_ref
  54.8 41.0 %all-to-all-done.1.rows_ref = bf16[128,48,128]{2,1,0:T(8,128)(2,1)S(1)} async-done(((bf16[128,48,128]{2,1,0:T(8,128)(2,1)}), bf16[128,48,128]{2,1,0:T(8,128)(2,1)S(1)}, u32[]{:S(2)}, u32[]{:S(2)}) %all-to-all-start.1) | async-done | bytes 1572896 | tf_op jit(solution)/shard_map/all_to_all | solution.py:304
  95.8 6.0 %accumulate.1 = (f32[28,28,768]{2,1,0:T(8,128)}, f32[28,1,768]{2,1,0:T(1,128)S(1)}) custom-call(bf16[128,48,128]{2,1,0:T(8,128)(2,1)S(1)} %all-to-all-done.1.rows_ref, s32[128,12]{1,0:T(8,128)S(1)} %reshape.20.recv_ref), custom_call_target="tpu_custom_call" | custom-call | tf_op jit(solution)/shard_map/accumulate/pallas_call | solution.py:308
  101.8 0.6 copy.32
  (5 shorter events, 0.1 us)
Async XLA Ops:
  0.6 14.8 %copy-start.3 = (f32[28,28]{1,0:T(8,128)S(1)}, f32[28,28]{1,0:T(8,128)}, u32[]{:S(2)}) copy-start(f32[28,28]{1,0:T(8,128)} %mass_ref.3) | copy-start | bytes 9412
  0.6 14.8 %copy-start.4 = (s32[4,128]{1,0:T(4,128)S(1)}, s32[4,128]{1,0:T(4,128)}, u32[]{:S(2)}) copy-start(s32[4,128]{1,0:T(4,128)} %send_ref.3) | copy-start | bytes 6148
  0.7 14.8 %copy-start = (bf16[84,84,128]{2,1,0:T(8,128)(2,1)S(1)}, bf16[84,84,128]{2,1,0:T(8,128)(2,1)}, u32[]{:S(2)}) copy-start(bf16[84,84,128]{2,1,0:T(8,128)(2,1)} %ainv_ref.3) | copy-start | bytes 5419012
  2.4 13.1 %all-to-all-start = ((f32[4,32,128]{2,1,0:T(8,128)}), f32[4,32,128]{2,1,0:T(8,128)S(1)}, u32[]{:S(2)}, u32[]{:S(2)}) async-start(f32[4,32,128]{2,1,0:T(8,128)} %bitcast.11), calls=%async_computation | async-start | bytes 131072 | tf_op jit(solution)/shard_map/all_to_all | solution.py:252
  15.5 1.0 copy-start.1
  16.5 1.0 copy-start.2
  36.7 18.0 %copy-start.5 = (s32[1536]{0:T(1024)S(1)}, s32[1536]{0:T(1024)}, u32[]{:S(2)}) copy-start(s32[1536]{0:T(1024)} %param.26) | copy-start | bytes 18436
  36.7 59.1 %all-to-all-start.1 = ((bf16[128,48,128]{2,1,0:T(8,128)(2,1)}), bf16[128,48,128]{2,1,0:T(8,128)(2,1)S(1)}, u32[]{:S(2)}, u32[]{:S(2)}) async-start(bf16[128,48,128]{2,1,0:T(8,128)(2,1)} %get-tuple-element.13), calls=%async_computation.1 | async-start | bytes 3145728 | tf_op jit(solution)/shard_map/all_to_all | solution.py:304

commit v2 on v1

--- a/solution.py
+++ b/solution.py
@@ -14,9 +14,10 @@
 NF_LO = 10
 NI_LO = 20
 LO_PAD = 16
-LO_STRIDE = 12
 HI_PAD = 32
-HI_STRIDE = 32
+SKEW = 4
+UNROLL = 2
+UNROLL_C = 1
 NT = (((1,), (1,)), ((), ()))
 TN = (((0,), (0,)), ((), ()))
 VMEM = pl.BlockSpec(memory_space=pltpu.VMEM)
@@ -35,9 +36,10 @@
 
 def condense_body(
     ainv_ref, geom, load, degree, lift_ref, trace_ref, mass_ref, part_ref,
-    lmat, solved, masked, rhs_load, stack, massb, width, inner, pad, stride, rows
+    lmat, solved, masked, rhs_load, stack, massb, width, inner, pad, rows
 ):
     am = 4 * width
+    depth = trace_ref.shape[1] // TERMS
     inner_mask, face_mask = masks(degree, inner, pad)
     masked[...] = inner_mask
     rhs_load[...] = load * inner_mask
@@ -45,49 +47,55 @@
         for a in range(4):
             piece = lift_ref[t, a][:width, :inner]
             piece = jnp.concatenate([piece, jnp.zeros((pad - width, inner), F32)], axis=0)
-            lmat[a, t * pad:(t + 1) * pad, :] = piece.astype(BF16)
+            for g in range(pad // 8):
+                at = (g * TERMS + t) * 8
+                lmat[a, at:at + 8, :] = piece[g * 8:(g + 1) * 8].astype(BF16)
     mass = mass_ref[...][:width, :width]
     mass = jnp.concatenate([mass, jnp.zeros((pad - width, width), F32)], axis=0)
     for m in range(width):
         massb[m] = jnp.broadcast_to(mass[:, m:m + 1], (pad, LANES))
+
+    def combined(out, k, g, scales):
+        total = None
+        for t in range(TERMS):
+            at = (g * TERMS + t) * 8
+            term = out[at:at + 8, k * LANES:(k + 1) * LANES] * scales[t]
+            total = term if total is None else total + term
+        return total
+
     trace_g = [geom[TERMS + t:TERMS + t + 1, :] for t in range(TERMS)]
 
+    filler = jnp.zeros((depth - inner, LANES), F32)
+
     def solve(pair, carry):
-        blocks = []
-        rows_mask = []
+        columns = []
         for k in range(2):
             j = 2 * pair + k
             block = ainv_ref[j].astype(F32)
             row_mask = masked[pl.ds(j, 1), :]
             part_ref[pl.ds(j, 1), :] = row_mask * jnp.sum(block * rhs_load[...], axis=0, keepdims=True)
-            blocks.append((block * masked[...]).astype(BF16))
-            rows_mask.append(row_mask)
-        out = jnp.dot(trace_ref[...], jnp.concatenate(blocks, axis=1), preferred_element_type=F32)
+            block = block * masked[...]
+            stacked = []
+            for t in range(TERMS):
+                stacked += [block * (trace_g[t] * row_mask), filler]
+            columns.append(jnp.concatenate(stacked, axis=0).astype(BF16))
+        out = jnp.dot(trace_ref[...], jnp.concatenate(columns, axis=1), preferred_element_type=F32)
         for k in range(2):
-            j = 2 * pair + k
-            total = None
-            for t in range(TERMS):
-                term = out[t * am:(t + 1) * am, k * LANES:(k + 1) * LANES] * (trace_g[t] * rows_mask[k])
-                total = term if total is None else total + term
-            solved[pl.ds(pl.multiple_of(j * am, 8), am), :] = total
+            solved[pl.ds(2 * pair + k, am, stride=inner), :] = out[:, k * LANES:(k + 1) * LANES]
         return carry
 
-    lax.fori_loop(0, inner // 2, solve, 0)
-
-    lift_g = [geom[t:t + 1, :] for t in range(TERMS)]
+    lax.fori_loop(0, inner // 2, solve, 0, unroll=UNROLL)
+
+    lift_g = [jnp.broadcast_to(geom[t:t + 1, :], (8, LANES)) for t in range(TERMS)]
 
     def mixed(out, k):
-        total = None
-        for t in range(TERMS):
-            term = out[t * pad:(t + 1) * pad, k * LANES:(k + 1) * LANES] * lift_g[t]
-            total = term if total is None else total + term
-        return total
+        return jnp.concatenate([combined(out, k, g, lift_g) for g in range(pad // 8)], axis=0)
 
     part = part_ref[...].astype(BF16)
     for a in range(4):
         out = jnp.dot(lmat[a], part, preferred_element_type=F32)
         value = -(mixed(out, 0) * face_mask)
-        stack[pl.ds(a * rows + width, width, stride=stride), :] = value[:width]
+        stack[a * rows + width * width:a * rows + width * width + width, :] = value[:width]
     scales = [geom[2 * TERMS + a:2 * TERMS + a + 1, :] for a in range(4)]
 
     def couple(pair, carry):
@@ -95,16 +103,16 @@
             columns = []
             for k in range(2):
                 m = 2 * pair + k
-                columns.append(solved[pl.ds(a * width + m, inner, stride=am), :].astype(BF16))
+                columns.append(solved[pl.ds((a * width + m) * inner, inner), :].astype(BF16))
             out = jnp.dot(lmat[a], jnp.concatenate(columns, axis=1), preferred_element_type=F32)
             for k in range(2):
                 m = 2 * pair + k
                 column_mask = (m.astype(F32) < (degree + 1.0) * (degree + 2.0) / 2.0).astype(F32)
                 value = (massb[m] * scales[a] - mixed(out, k)) * (face_mask * column_mask)
-                stack[pl.ds(a * rows + m, width, stride=stride), :] = value[:width]
+                stack[pl.ds(a * rows + m * width, width), :] = value[:width]
         return carry
 
-    lax.fori_loop(0, width // 2, couple, 0)
+    lax.fori_loop(0, width // 2, couple, 0, unroll=UNROLL_C)
 
 
 def one_hots(send_ref, chosen, capacity):
@@ -136,7 +144,7 @@
     condense_body(
         ainv_ref, geom_ref[...], load_ref[...].astype(F32), degree_ref[...].astype(F32), lift_ref, trace_ref,
         mass_ref, part_ref, lmat, solved, masked, rhs_load, stack, massb,
-        NF_LO, NI_LO, LO_PAD, LO_STRIDE, LANES,
+        NF_LO, NI_LO, LO_PAD, LANES,
     )
     one_hots(send_ref, chosen, capacity)
     for a in range(4):
@@ -150,62 +158,74 @@
 ):
     inner = ainv_ref.shape[0]
     width = mass_ref.shape[0]
-    tiles = width * HI_STRIDE // LANES
     groups = out_ref.shape[0]
     per = out_ref.shape[1]
+    tiles = per // capacity - 1
+    rows = tiles * LANES
+    step = per + SKEW
     rec[...] = record_ref[...].T
     geom = rec[inner:inner + 12, :]
     degree = rec[inner + 12:inner + 13, :]
-    stack[...] = jnp.zeros_like(stack)
+    used = width * (width + 1)
+    for a in range(4):
+        stack[a * rows + used:(a + 1) * rows, :] = jnp.zeros((rows - used, LANES), F32)
     condense_body(
         ainv_ref, geom, rec[:inner, :], degree, lift_ref, trace_ref, mass_ref, part_ref,
         lmat, solved, masked, rhs_load, stack, massb,
-        width, inner, HI_PAD, HI_STRIDE, width * HI_STRIDE,
+        width, inner, HI_PAD, rows,
     )
     one_hots(send_ref, chosen, capacity)
-    rows = width * HI_STRIDE
     for c in range(capacity):
-        wide[pl.ds(c * (tiles + 1) + tiles, groups, stride=per), :] = low_ref[c * groups:(c + 1) * groups, :]
-
-    def place(q, carry):
-        for a in range(4):
-            piece = stack[pl.ds(pl.multiple_of(a * rows + q * LANES, LANES), LANES), :]
-            rowsb[:, a * LANES:(a + 1) * LANES] = piece.astype(BF16)
-        got = lax.dot_general(chosen[...], rowsb[...], NT, preferred_element_type=F32)
-        for c in range(capacity):
-            wide[pl.ds(c * (tiles + 1) + q, groups, stride=per), :] = got[c * groups:(c + 1) * groups, :]
+        wide[pl.ds(tiles * capacity + c, groups, stride=step), :] = low_ref[c * groups:(c + 1) * groups, :]
+
+    def place(q, count):
+        for k in range(count):
+            for a in range(4):
+                piece = stack[pl.ds(pl.multiple_of(a * rows + (q + k) * LANES, LANES), LANES), :]
+                rowsb[k * LANES:(k + 1) * LANES, a * LANES:(a + 1) * LANES] = piece.astype(BF16)
+        got = lax.dot_general(chosen[...], rowsb[:count * LANES], NT, preferred_element_type=F32)
+        for k in range(count):
+            for c in range(capacity):
+                wide[pl.ds((q + k) * capacity + c, groups, stride=step), :] = (
+                    got[c * groups:(c + 1) * groups, k * LANES:(k + 1) * LANES]
+                )
+
+    def place_pair(pair, carry):
+        place(2 * pair, 2)
         return carry
 
-    lax.fori_loop(0, tiles, place, 0)
+    lax.fori_loop(0, tiles // 2, place_pair, 0)
+    if tiles % 2:
+        place(tiles - 1, 1)
 
     def narrow(o, carry):
-        out_ref[o] = wide[pl.ds(pl.multiple_of(o * per, 8), per), :].astype(BF16)
+        out_ref[o] = wide[pl.ds(o * step, per), :].astype(BF16)
         return carry
 
-    lax.fori_loop(0, groups, narrow, 0)
-
-
-def accumulate_kernel(capacity, rows_ref, recv_ref, blocks_ref, rhs_ref, wide, hot_lo, hot_hi, low_sum, rhs_sum):
+    lax.fori_loop(0, groups, narrow, 0, unroll=4)
+
+
+def accumulate_kernel(capacity, width, rows_ref, recv_ref, blocks_ref, rhs_ref, wide, hot_lo, hot_hi, low_sum, total):
     q = pl.program_id(0)
     groups, per, _ = rows_ref.shape
     faces = blocks_ref.shape[2]
     tiles = per // capacity - 1
-    width = blocks_ref.shape[1]
-    per_tile = LANES // HI_STRIDE
+    rows = tiles * LANES
+    step = per + SKEW
 
     def gathered(at):
         pieces = [
-            wide[pl.ds(c * (tiles + 1) + at, groups, stride=per), :].astype(BF16) for c in range(capacity)
+            wide[pl.ds(at * capacity + c, groups, stride=step), :].astype(BF16) for c in range(capacity)
         ]
         return jnp.concatenate(pieces, axis=0)
 
     @pl.when(q == 0)
     def _():
         def widen(g, carry):
-            wide[pl.ds(pl.multiple_of(g * per, 8), per), :] = rows_ref[g].astype(F32)
+            wide[pl.ds(g * step, per), :] = rows_ref[g].astype(F32)
             return carry
 
-        lax.fori_loop(0, groups, widen, 0)
+        lax.fori_loop(0, groups, widen, 0, unroll=4)
         columns = lax.broadcasted_iota(jnp.int32, (groups, faces), 1)
         for c in range(capacity):
             hot_lo[c * groups:(c + 1) * groups, :] = (recv_ref[:, c:c + 1] == columns).astype(F32).astype(BF16)
@@ -214,19 +234,30 @@
             )
         low_sum[...] = lax.dot_general(gathered(tiles), hot_lo[...], TN, preferred_element_type=F32)
 
-    total = lax.dot_general(gathered(q), hot_hi[...], TN, preferred_element_type=F32)
-    for k in range(per_tile):
-        blocks_ref[k] = total[k * HI_STRIDE:k * HI_STRIDE + width, :]
-        rhs_ref[k] = total[k * HI_STRIDE + width:k * HI_STRIDE + width + 1, :]
-    for s in range(-(-NF_LO // per_tile)):
-        @pl.when(q == s)
-        def _():
-            for k in range(per_tile):
-                i = s * per_tile + k
-                if i < NF_LO:
-                    low = low_sum[i * LO_STRIDE:i * LO_STRIDE + NF_LO + 1, :]
-                    blocks_ref[k, :NF_LO, :] = blocks_ref[k, :NF_LO, :] + low[:NF_LO]
-                    rhs_ref[k] = rhs_ref[k] + low[NF_LO:NF_LO + 1]
+    @pl.when(q < tiles)
+    def _():
+        got = lax.dot_general(gathered(q), hot_hi[...], TN, preferred_element_type=F32)
+        for f in range(faces // LANES):
+            total[pl.ds(pl.multiple_of(f * rows + q * LANES, LANES), LANES), :] = got[:, f * LANES:(f + 1) * LANES]
+
+    @pl.when(q == tiles - 1)
+    def _():
+        for m in range(NF_LO + 1):
+            for f in range(faces // LANES):
+                at = f * rows + (m if m < NF_LO else width) * width
+                total[at:at + NF_LO, :] = (
+                    total[at:at + NF_LO, :] + low_sum[m * NF_LO:(m + 1) * NF_LO, f * LANES:(f + 1) * LANES]
+                )
+        for f in range(faces // LANES):
+            at = f * rows + width * width
+            rhs_ref[:, f * LANES:(f + 1) * LANES] = total[at:at + width, :]
+
+    @pl.when(q >= tiles)
+    def _():
+        for k in range(blocks_ref.shape[0]):
+            i = (q - tiles) * blocks_ref.shape[0] + k
+            for f in range(faces // LANES):
+                blocks_ref[k, :, f * LANES:(f + 1) * LANES] = total[pl.ds(f * rows + i, width, stride=width), :]
 
 
 def on_device(
@@ -237,9 +268,9 @@
     inner, _, elements = hi_ainv.shape
     groups = lax.axis_size("geo")
     capacity = 6 * lo_ainv.shape[2] // groups
-    tiles = width * HI_STRIDE // LANES
+    tiles = -(-width * (width + 1) // LANES)
+    rows = tiles * LANES
     per = capacity * (tiles + 1)
-    rows = width * HI_STRIDE
     faces = groups * capacity
 
     record = pl.pallas_call(
@@ -252,8 +283,14 @@
     record = lax.all_to_all(record, "deg", split_axis=0, concat_axis=0, tiled=True)
 
     turned = jnp.transpose(trace_ref, (0, 2, 3, 1))
-    trace_hi = turned.reshape(TERMS * 4 * width, inner).astype(BF16)
-    trace_lo = turned[:, :, :NF_LO, :NI_LO].reshape(TERMS * 4 * NF_LO, NI_LO).astype(BF16)
+
+    def stacked(operator):
+        wide = -(-operator.shape[3] // 8) * 8
+        operator = jnp.pad(operator, ((0, 0), (0, 0), (0, 0), (0, wide - operator.shape[3])))
+        return jnp.transpose(operator, (1, 2, 0, 3)).reshape(-1, TERMS * wide).astype(BF16)
+
+    trace_hi = stacked(turned)
+    trace_lo = stacked(turned[:, :, :NF_LO, :NI_LO])
 
     low_particular, placed = pl.pallas_call(
         functools.partial(low_kernel, capacity),
@@ -293,9 +330,9 @@
             pltpu.VMEM((4 * rows, LANES), F32),
             pltpu.VMEM((width, HI_PAD, LANES), F32),
             pltpu.VMEM((groups * capacity, 4 * LANES), BF16),
-            pltpu.VMEM((LANES, 4 * LANES), BF16),
+            pltpu.VMEM((2 * LANES, 4 * LANES), BF16),
             pltpu.VMEM((LANES, LANES), F32),
-            pltpu.VMEM((groups * per, LANES), F32),
+            pltpu.VMEM((groups * (per + SKEW), LANES), F32),
         ],
         compiler_params=pltpu.CompilerParams(vmem_limit_bytes=48 << 20),
         name="high",
@@ -304,33 +341,33 @@
     arrived = lax.all_to_all(outgoing, "geo", split_axis=0, concat_axis=0, tiled=True)
 
     plan = recv_face.reshape(groups, 2 * capacity)
-    per_tile = LANES // HI_STRIDE
+    share = width // 7
     blocks, right = pl.pallas_call(
-        functools.partial(accumulate_kernel, capacity),
+        functools.partial(accumulate_kernel, capacity, width),
         out_shape=(
             jax.ShapeDtypeStruct((width, width, faces), F32),
-            jax.ShapeDtypeStruct((width, 1, faces), F32),
+            jax.ShapeDtypeStruct((width, faces), F32),
         ),
-        grid=(tiles,),
+        grid=(tiles + 7,),
         in_specs=[
             pl.BlockSpec((groups, per, LANES), lambda q: (0, 0, 0)),
             pl.BlockSpec((groups, 2 * capacity), lambda q: (0, 0)),
         ],
         out_specs=(
-            pl.BlockSpec((per_tile, width, faces), lambda q: (q, 0, 0)),
-            pl.BlockSpec((per_tile, 1, faces), lambda q: (q, 0, 0)),
+            pl.BlockSpec((share, width, faces), lambda q: (jnp.maximum(q - tiles, 0), 0, 0)),
+            pl.BlockSpec((width, faces), lambda q: (0, 0)),
         ),
         scratch_shapes=[
-            pltpu.VMEM((groups * per, LANES), F32),
+            pltpu.VMEM((groups * (per + SKEW), LANES), F32),
             pltpu.VMEM((groups * capacity, faces), BF16),
             pltpu.VMEM((groups * capacity, faces), BF16),
             pltpu.VMEM((LANES, faces), F32),
-            pltpu.VMEM((8, LANES), F32),
+            pltpu.VMEM((faces // LANES * rows, LANES), F32),
         ],
         compiler_params=pltpu.CompilerParams(vmem_limit_bytes=48 << 20),
         name="accumulate",
     )(arrived, plan)
-    return (low_particular, high_particular, blocks, right.reshape(width, faces))
+    return (low_particular, high_particular, blocks, right)
 
 
 def solution(mesh):

time: 103 us -> 95.9 us (0.931)
  Pallas kernels: 31.8 us -> 24.7 us
    pallas_call x1, Pallas kernels: 19.3 us -> 12.2 us  [on_device(): pl.pallas_call(functools.partial(high_kernel, capacity), out_shape=(jax.S...]
    unnamed x14 -> x13, local copies, waits for them, and re-layouts: 4.28 us -> 3.63 us
  transfers between devices with their start and end apart: 2 -> 2, of which waited for: 1 -> 1; matrix products, arithmetic and copies ran while one was open for 3% -> 4% of each run, Pallas kernels for 5% -> 4%
where the time goes in v2:
time: 95.9 us; the launch traced here: 95 us
  waiting for transfers between devices  41 us (43%)
  Pallas kernels  24.7 us (26%)
  starting transfers between devices  22.8 us (24%)
  local copies, waits for them, and re-layouts  4.72 us (5%)
  other arithmetic  0.98 us (1%)
    all_to_all x1, waiting for transfers between devices, on_device(): lax.all_to_all(outgoing, 'geo', split_axis=0, concat_axis=0, tiled=True)  41 us
    all_to_all x1, starting transfers between devices, on_device(): lax.all_to_all(outgoing, 'geo', split_axis=0, concat_axis=0, tiled=True)  18 us
    pallas_call x1, Pallas kernels, on_device(): pl.pallas_call(functools.partial(high_kernel, capacity), out_shape=(jax.S...  12.2 us
    pallas_call x1, Pallas kernels, on_device(): pl.pallas_call(functools.partial(accumulate_kernel, capacity, width), out...  6.82 us
    all_to_all x1, starting transfers between devices, on_device(): lax.all_to_all(record, 'deg', split_axis=0, concat_axis=0, tiled=True)  4.84 us
    pallas_call x1, Pallas kernels, on_device(): pl.pallas_call(functools.partial(low_kernel, capacity), out_shape=(jax.Sh...  4.01 us
    unnamed x13, local copies, waits for them, and re-layouts  3.63 us
  transfers between devices with their start and end apart: 2, of which 1 were waited for; matrix products, arithmetic and copies ran while one was open for 4% of the time, Pallas kernels for 4%

profile of v2, /device:TPU:1, one launch (start us, length us, event | category | flops | bytes accessed | tf_op | source)
XLA Modules:
  0.0 95.0 jit_solution(14405848013534688925)
XLA Ops:
  0.6 0.0 copy-start.3
  0.6 0.0 copy-start.4
  0.7 0.0 copy-start
  0.7 1.7 %record.1 = f32[128,128]{1,0:T(8,128)} custom-call(f32[12,128]{1,0:T(8,128)} %geom_ref.3, bf16[84,128]{1,0:T(8,128)(2,1)} %load_ref.3, s32[1,128]{1,0:T(1,128)} %bitcast.13, s32[1,128]{1,0:T(1,128)} %bitcast.14), custom_call_target="tpu_custom_call" | custom-call | tf_op jit(solution)/shard_map/record/pallas_call | solution.py:276
  2.4 4.8 %all-to-all-start = ((f32[4,32,128]{2,1,0:T(8,128)}), f32[4,32,128]{2,1,0:T(8,128)S(1)}, u32[]{:S(2)}, u32[]{:S(2)}) async-start(f32[4,32,128]{2,1,0:T(8,128)} %bitcast.12), calls=%async_computation | async-start | bytes 131072 | tf_op jit(solution)/shard_map/all_to_all | solution.py:283
  7.2 1.0 %convert_bitcast_fusion = bf16[4,4,28,84]{3,1,2,0:T(4,128)(2,1)S(1)} fusion(f32[4,84,4,28]{1,2,3,0:T(4,128)} %param.28), kind=kLoop, calls=%fused_computation | loop fusion | flops 37632 | bytes 225792 | tf_op jit(solution)/shard_map/convert.4
  8.2 0.1 pad_bitcast_fusion
  8.4 0.1 convert_element_type.17.trace_ref
  8.6 0.7 convert_element_type.15.trace_ref
  9.3 1.7 %copy.24.lift_ref = f32[4,4,28,84]{3,2,1,0:T(8,128)} copy(f32[4,4,28,84]{3,1,2,0:T(4,128)} %param.27) | data formatting | bytes 301056 | tf_op args[12]
  10.9 4.0 %low.1 = (f32[20,128]{1,0:T(8,128)}, f32[768,128]{1,0:T(8,128)}) custom-call(bf16[20,20,128]{2,1,0:T(8,128)(2,1)} %ainv_ref.2, f32[12,128]{1,0:T(8,128)} %geom_ref.2, bf16[20,128]{1,0:T(8,128)(2,1)} %load_ref.2, s32[1,128]{1,0:T(1,128)} %bitcast.15, s32[4,128]{1,0:T(4,128)} %send_ref.2, f32[4,4,28,84]{3,2,1,0:T(8,128)} %copy.24.lift_ref, ...), custom_call_target="tpu_custom_call" | custom-call | flops 400000000 | bytes 2000000 | tf_op jit(solution)/shard_map/low/pallas_call | solution.py:295
  14.9 0.0 all-to-all-done
  14.9 0.0 copy-done.3
  15.0 0.0 copy-done.4
  15.0 0.0 copy-done
  15.0 0.0 copy-start.1
  15.0 0.9 copy-done.1
  15.9 1.0 %copy-done.2 = f32[768,128]{1,0:T(8,128)S(1)} copy-done((f32[768,128]{1,0:T(8,128)S(1)}, f32[768,128]{1,0:T(8,128)}, u32[]{:S(2)}) %copy-start.2) | copy-done | bytes 393240
  16.9 12.2 %high.1 = (f32[84,128]{1,0:T(8,128)}, bf16[128,48,128]{2,1,0:T(8,128)(2,1)}) custom-call(bf16[84,84,128]{2,1,0:T(8,128)(2,1)S(1)} %copy-done, f32[128,128]{1,0:T(8,128)S(1)} %bitcast.11, s32[4,128]{1,0:T(4,128)S(1)} %copy-done.4, f32[4,4,28,84]{3,2,1,0:T(8,128)S(1)} %copy-done.1, bf16[112,352]{1,0:T(8,128)(2,1)S(1)} %convert_element_type.17.trace_ref, ...), custom_call_target="tpu_custom_call" | custom-call | tf_op jit(solution)/shard_map/high/pallas_call | solution.py:317
  29.1 18.0 %all-to-all-start.1 = ((bf16[128,48,128]{2,1,0:T(8,128)(2,1)}), bf16[128,48,128]{2,1,0:T(8,128)(2,1)S(1)}, u32[]{:S(2)}, u32[]{:S(2)}) async-start(bf16[128,48,128]{2,1,0:T(8,128)(2,1)} %get-tuple-element.13), calls=%async_computation.1 | async-start | bytes 3145728 | tf_op jit(solution)/shard_map/all_to_all | solution.py:341
  47.1 0.0 copy-done.5
  47.1 0.1 reshape.17.recv_ref
  47.2 41.0 %all-to-all-done.1.rows_ref = bf16[128,48,128]{2,1,0:T(8,128)(2,1)S(1)} async-done(((bf16[128,48,128]{2,1,0:T(8,128)(2,1)}), bf16[128,48,128]{2,1,0:T(8,128)(2,1)S(1)}, u32[]{:S(2)}, u32[]{:S(2)}) %all-to-all-start.1) | async-done | bytes 1572896 | tf_op jit(solution)/shard_map/all_to_all | solution.py:341
  88.2 6.8 %accumulate.1 = (f32[28,28,768]{2,1,0:T(8,128)}, f32[28,768]{1,0:T(8,128)}) custom-call(bf16[128,48,128]{2,1,0:T(8,128)(2,1)S(1)} %all-to-all-done.1.rows_ref, s32[128,12]{1,0:T(8,128)S(1)} %reshape.17.recv_ref), custom_call_target="tpu_custom_call" | custom-call | tf_op jit(solution)/shard_map/accumulate/pallas_call | solution.py:345
  (6 shorter events, 0.1 us)
Async XLA Ops:
  0.6 14.3 %copy-start.3 = (f32[28,28]{1,0:T(8,128)S(1)}, f32[28,28]{1,0:T(8,128)}, u32[]{:S(2)}) copy-start(f32[28,28]{1,0:T(8,128)} %mass_ref.3) | copy-start | bytes 9412
  0.6 14.3 %copy-start.4 = (s32[4,128]{1,0:T(4,128)S(1)}, s32[4,128]{1,0:T(4,128)}, u32[]{:S(2)}) copy-start(s32[4,128]{1,0:T(4,128)} %send_ref.3) | copy-start | bytes 6148
  0.7 14.3 %copy-start = (bf16[84,84,128]{2,1,0:T(8,128)(2,1)S(1)}, bf16[84,84,128]{2,1,0:T(8,128)(2,1)}, u32[]{:S(2)}) copy-start(bf16[84,84,128]{2,1,0:T(8,128)(2,1)} %ainv_ref.3) | copy-start | bytes 5419012
  2.4 12.5 %all-to-all-start = ((f32[4,32,128]{2,1,0:T(8,128)}), f32[4,32,128]{2,1,0:T(8,128)S(1)}, u32[]{:S(2)}, u32[]{:S(2)}) async-start(f32[4,32,128]{2,1,0:T(8,128)} %bitcast.12), calls=%async_computation | async-start | bytes 131072 | tf_op jit(solution)/shard_map/all_to_all | solution.py:283
  15.0 1.0 %copy-start.1 = (f32[4,4,28,84]{3,2,1,0:T(8,128)S(1)}, f32[4,4,28,84]{3,2,1,0:T(8,128)}, u32[]{:S(2)}) copy-start(f32[4,4,28,84]{3,2,1,0:T(8,128)} %copy.24.lift_ref) | copy-start | bytes 451588
  15.9 1.0 %copy-start.2 = (f32[768,128]{1,0:T(8,128)S(1)}, f32[768,128]{1,0:T(8,128)}, u32[]{:S(2)}) copy-start(f32[768,128]{1,0:T(8,128)} %get-tuple-element.11.low_ref) | copy-start | bytes 1179652
  29.1 18.0 %copy-start.5 = (s32[1536]{0:T(1024)S(1)}, s32[1536]{0:T(1024)}, u32[]{:S(2)}) copy-start(s32[1536]{0:T(1024)} %param.26) | copy-start | bytes 18436
  29.1 59.1 %all-to-all-start.1 = ((bf16[128,48,128]{2,1,0:T(8,128)(2,1)}), bf16[128,48,128]{2,1,0:T(8,128)(2,1)S(1)}, u32[]{:S(2)}, u32[]{:S(2)}) async-start(bf16[128,48,128]{2,1,0:T(8,128)(2,1)} %get-tuple-element.13), calls=%async_computation.1 | async-start | bytes 3145728 | tf_op jit(solution)/shard_map/all_to_all | solution.py:341

commit v3 on v2

--- a/solution.py
+++ b/solution.py
@@ -21,6 +21,9 @@
 NT = (((1,), (1,)), ((), ()))
 TN = (((0,), (0,)), ((), ()))
 VMEM = pl.BlockSpec(memory_space=pltpu.VMEM)
+ANY = pl.BlockSpec(memory_space=pl.ANY)
+MESH = pl.DeviceIdType.MESH
+LOW_ROWS = 8
 
 
 def masks(degree, inner_width, face_width):
@@ -36,7 +39,7 @@
 
 def condense_body(
     ainv_ref, geom, load, degree, lift_ref, trace_ref, mass_ref, part_ref,
-    lmat, solved, masked, rhs_load, stack, massb, width, inner, pad, rows
+    lmat, solved, masked, rhs_load, stack, massb, width, inner, pad, rows, between=None
 ):
     am = 4 * width
     depth = trace_ref.shape[1] // TERMS
@@ -85,6 +88,8 @@
         return carry
 
     lax.fori_loop(0, inner // 2, solve, 0, unroll=UNROLL)
+    if between is not None:
+        between()
 
     lift_g = [jnp.broadcast_to(geom[t:t + 1, :], (8, LANES)) for t in range(TERMS)]
 
@@ -138,8 +143,10 @@
 
 def low_kernel(
     capacity, ainv_ref, geom_ref, load_ref, degree_ref, send_ref, lift_ref, trace_ref, mass_ref,
-    part_ref, placed_ref, lmat, solved, masked, rhs_load, stack, massb, chosen, rowsb
+    part_ref, out_ref, lmat, solved, masked, rhs_load, stack, massb, chosen, rowsb, wide
 ):
+    groups = out_ref.shape[0]
+    step = LOW_ROWS + SKEW
     stack[...] = jnp.zeros_like(stack)
     condense_body(
         ainv_ref, geom_ref[...], load_ref[...].astype(F32), degree_ref[...].astype(F32), lift_ref, trace_ref,
@@ -149,69 +156,133 @@
     one_hots(send_ref, chosen, capacity)
     for a in range(4):
         rowsb[:, a * LANES:(a + 1) * LANES] = stack[a * LANES:(a + 1) * LANES, :].astype(BF16)
-    placed_ref[...] = lax.dot_general(chosen[...], rowsb[...], NT, preferred_element_type=F32)
+    got = lax.dot_general(chosen[...], rowsb[...], NT, preferred_element_type=F32)
+    for c in range(capacity):
+        wide[pl.ds(c, groups, stride=step), :] = got[c * groups:(c + 1) * groups, :]
+    for c in range(capacity, LOW_ROWS):
+        wide[pl.ds(c, groups, stride=step), :] = jnp.zeros((groups, LANES), F32)
+
+    def narrow(o, carry):
+        out_ref[o] = wide[pl.ds(o * step, LOW_ROWS), :].astype(BF16)
+        return carry
+
+    lax.fori_loop(0, groups, narrow, 0, unroll=4)
+
+
+def peer_at(me, k, groups):
+    j = lax.rem(k * 37, groups)
+    side = 8 if groups % 16 == 0 else 1
+    outer = groups // (2 * side)
+    y = lax.rem(me // (2 * side) + j // (2 * side), outer)
+    z = lax.rem(lax.rem(me // 2, side) + lax.rem(j // 2, side), side)
+    core = lax.rem(me + j, 2)
+    return (y * side + z) * 2 + core
 
 
 def high_kernel(
     capacity, ainv_ref, record_ref, send_ref, lift_ref, trace_ref, mass_ref, low_ref,
-    part_ref, out_ref, lmat, solved, masked, rhs_load, stack, massb, chosen, rowsb, rec, wide
+    part_ref, rows_ref, low_rows_ref, lmat, solved, masked, rhs_load, stack, massb, chosen, rowsb, rec, wide, outgoing,
+    send_sem, recv_sem, own_sem
 ):
     inner = ainv_ref.shape[0]
     width = mass_ref.shape[0]
-    groups = out_ref.shape[0]
-    per = out_ref.shape[1]
-    tiles = per // capacity - 1
+    groups, per, _ = rows_ref.shape
+    used = width * (width + 1)
+    full = used // LANES
+    tiles = full + 1
     rows = tiles * LANES
     step = per + SKEW
+    half = LANES // 2
+    me = lax.axis_index("geo")
+    barrier = pltpu.get_barrier_semaphore()
+
+    def greet(k, carry):
+        pl.semaphore_signal(barrier, inc=1, device_id={"geo": peer_at(me, k, groups)}, device_id_type=MESH)
+        return carry
+
+    lax.fori_loop(1, groups, greet, 0)
+
+    def send_all(source, target, at):
+        def send(k, carry):
+            peer = peer_at(me, k, groups)
+            pltpu.make_async_remote_copy(
+                src_ref=source.at[peer], dst_ref=target.at[me], send_sem=send_sem.at[at], recv_sem=recv_sem.at[at],
+                device_id={"geo": peer}, device_id_type=MESH,
+            ).start()
+            return carry
+
+        lax.fori_loop(1, groups, send, 0)
+        pltpu.make_async_copy(source.at[me], target.at[me], own_sem.at[at]).start()
+
+    def wait_all(source, target, at):
+        pltpu.make_async_copy(source.at[me], target.at[me], own_sem.at[at]).wait()
+        sent = source.at[pl.ds(0, groups - 1)]
+        pltpu.make_async_copy(sent, sent, send_sem.at[at]).wait()
+        come = target.at[pl.ds(0, groups - 1)]
+        pltpu.make_async_copy(come, come, recv_sem.at[at]).wait()
+
+    def between():
+        pl.semaphore_wait(barrier, groups - 1)
+        send_all(low_ref, low_rows_ref, 0)
+
     rec[...] = record_ref[...].T
     geom = rec[inner:inner + 12, :]
     degree = rec[inner + 12:inner + 13, :]
-    used = width * (width + 1)
     for a in range(4):
         stack[a * rows + used:(a + 1) * rows, :] = jnp.zeros((rows - used, LANES), F32)
     condense_body(
         ainv_ref, geom, rec[:inner, :], degree, lift_ref, trace_ref, mass_ref, part_ref,
         lmat, solved, masked, rhs_load, stack, massb,
-        width, inner, HI_PAD, rows,
+        width, inner, HI_PAD, rows, between,
     )
     one_hots(send_ref, chosen, capacity)
-    for c in range(capacity):
-        wide[pl.ds(tiles * capacity + c, groups, stride=step), :] = low_ref[c * groups:(c + 1) * groups, :]
-
-    def place(q, count):
+
+    def placed(q, count):
         for k in range(count):
             for a in range(4):
                 piece = stack[pl.ds(pl.multiple_of(a * rows + (q + k) * LANES, LANES), LANES), :]
                 rowsb[k * LANES:(k + 1) * LANES, a * LANES:(a + 1) * LANES] = piece.astype(BF16)
-        got = lax.dot_general(chosen[...], rowsb[:count * LANES], NT, preferred_element_type=F32)
-        for k in range(count):
+        return lax.dot_general(chosen[...], rowsb[:count * LANES], NT, preferred_element_type=F32)
+
+    def place_pair(pair, carry):
+        got = placed(2 * pair, 2)
+        for k in range(2):
             for c in range(capacity):
-                wide[pl.ds((q + k) * capacity + c, groups, stride=step), :] = (
+                wide[pl.ds((2 * pair + k) * capacity + c, groups, stride=step), :] = (
                     got[c * groups:(c + 1) * groups, k * LANES:(k + 1) * LANES]
                 )
-
-    def place_pair(pair, carry):
-        place(2 * pair, 2)
-        return carry
-
-    lax.fori_loop(0, tiles // 2, place_pair, 0)
-    if tiles % 2:
-        place(tiles - 1, 1)
+        return carry
+
+    lax.fori_loop(0, full // 2, place_pair, 0)
+    tail = placed(full, 1)
+    for c in range(0, capacity, 2):
+        even = tail[c * groups:(c + 1) * groups, :]
+        odd = tail[(c + 1) * groups:(c + 2) * groups, :]
+        wide[pl.ds(full * capacity + c // 2, groups, stride=step), :] = even + pltpu.roll(odd, half, axis=1)
+    for r in range(full * capacity + capacity // 2, per):
+        wide[pl.ds(r, groups, stride=step), :] = jnp.zeros((groups, LANES), F32)
 
     def narrow(o, carry):
-        out_ref[o] = wide[pl.ds(o * step, per), :].astype(BF16)
+        outgoing[o] = wide[pl.ds(o * step, per), :].astype(BF16)
         return carry
 
     lax.fori_loop(0, groups, narrow, 0, unroll=4)
-
-
-def accumulate_kernel(capacity, width, rows_ref, recv_ref, blocks_ref, rhs_ref, wide, hot_lo, hot_hi, low_sum, total):
+    send_all(outgoing, rows_ref, 1)
+    wait_all(low_ref, low_rows_ref, 0)
+    wait_all(outgoing, rows_ref, 1)
+
+
+def accumulate_kernel(
+    capacity, width, rows_ref, low_ref, recv_ref, blocks_ref, rhs_ref, wide, low_wide, hot_lo, hot_hi, low_sum, total
+):
     q = pl.program_id(0)
     groups, per, _ = rows_ref.shape
     faces = blocks_ref.shape[2]
-    tiles = per // capacity - 1
+    full = width * (width + 1) // LANES
+    tiles = full + 1
     rows = tiles * LANES
     step = per + SKEW
+    low_step = LOW_ROWS + SKEW
 
     def gathered(at):
         pieces = [
@@ -219,10 +290,22 @@
         ]
         return jnp.concatenate(pieces, axis=0)
 
+    def tails():
+        pieces = []
+        for c in range(capacity):
+            piece = wide[pl.ds(full * capacity + c // 2, groups, stride=step), :]
+            pieces.append((pltpu.roll(piece, LANES // 2, axis=1) if c % 2 else piece).astype(BF16))
+        return jnp.concatenate(pieces, axis=0)
+
+    def lows():
+        pieces = [low_wide[pl.ds(c, groups, stride=low_step), :].astype(BF16) for c in range(capacity)]
+        return jnp.concatenate(pieces, axis=0)
+
     @pl.when(q == 0)
     def _():
         def widen(g, carry):
             wide[pl.ds(g * step, per), :] = rows_ref[g].astype(F32)
+            low_wide[pl.ds(g * low_step, LOW_ROWS), :] = low_ref[g].astype(F32)
             return carry
 
         lax.fori_loop(0, groups, widen, 0, unroll=4)
@@ -232,16 +315,20 @@
             hot_hi[c * groups:(c + 1) * groups, :] = (
                 (recv_ref[:, capacity + c:capacity + c + 1] == columns).astype(F32).astype(BF16)
             )
-        low_sum[...] = lax.dot_general(gathered(tiles), hot_lo[...], TN, preferred_element_type=F32)
-
-    @pl.when(q < tiles)
-    def _():
-        got = lax.dot_general(gathered(q), hot_hi[...], TN, preferred_element_type=F32)
+        low_sum[...] = lax.dot_general(lows(), hot_lo[...], TN, preferred_element_type=F32)
+
+    def add(pieces):
+        got = lax.dot_general(pieces, hot_hi[...], TN, preferred_element_type=F32)
         for f in range(faces // LANES):
             total[pl.ds(pl.multiple_of(f * rows + q * LANES, LANES), LANES), :] = got[:, f * LANES:(f + 1) * LANES]
 
-    @pl.when(q == tiles - 1)
+    @pl.when(q < full)
     def _():
+        add(gathered(q))
+
+    @pl.when(q == full)
+    def _():
+        add(tails())
         for m in range(NF_LO + 1):
             for f in range(faces // LANES):
                 at = f * rows + (m if m < NF_LO else width) * width
@@ -268,9 +355,10 @@
     inner, _, elements = hi_ainv.shape
     groups = lax.axis_size("geo")
     capacity = 6 * lo_ainv.shape[2] // groups
-    tiles = -(-width * (width + 1) // LANES)
+    full = width * (width + 1) // LANES
+    tiles = full + 1
     rows = tiles * LANES
-    per = capacity * (tiles + 1)
+    per = -(-(capacity * full + capacity // 2) // 8) * 8
     faces = groups * capacity
 
     record = pl.pallas_call(
@@ -296,7 +384,7 @@
         functools.partial(low_kernel, capacity),
         out_shape=(
             jax.ShapeDtypeStruct((NI_LO, elements), F32),
-            jax.ShapeDtypeStruct((groups * capacity, LANES), F32),
+            jax.ShapeDtypeStruct((groups, LOW_ROWS, LANES), BF16),
         ),
         in_specs=[VMEM] * 8,
         out_specs=(VMEM, VMEM),
@@ -309,19 +397,21 @@
             pltpu.VMEM((NF_LO, LO_PAD, LANES), F32),
             pltpu.VMEM((groups * capacity, 4 * LANES), BF16),
             pltpu.VMEM((LANES, 4 * LANES), BF16),
+            pltpu.VMEM((groups * (LOW_ROWS + SKEW), LANES), F32),
         ],
         cost_estimate=pl.CostEstimate(flops=400_000_000, bytes_accessed=2_000_000, transcendentals=0),
         name="low",
     )(lo_ainv, lo_geom, lo_load, lo_degree[None, :], lo_send, lift_ref, trace_lo, face_mass)
 
-    high_particular, outgoing = pl.pallas_call(
+    high_particular, arrived, low_arrived = pl.pallas_call(
         functools.partial(high_kernel, capacity),
         out_shape=(
             jax.ShapeDtypeStruct((inner, elements), F32),
             jax.ShapeDtypeStruct((groups, per, LANES), BF16),
+            jax.ShapeDtypeStruct((groups, LOW_ROWS, LANES), BF16),
         ),
-        in_specs=[VMEM] * 7,
-        out_specs=(VMEM, VMEM),
+        in_specs=[VMEM] * 6 + [ANY],
+        out_specs=(VMEM, ANY, ANY),
         scratch_shapes=[
             pltpu.VMEM((4, TERMS * HI_PAD, inner), BF16),
             pltpu.VMEM((inner * 4 * width, LANES), F32),
@@ -333,12 +423,14 @@
             pltpu.VMEM((2 * LANES, 4 * LANES), BF16),
             pltpu.VMEM((LANES, LANES), F32),
             pltpu.VMEM((groups * (per + SKEW), LANES), F32),
+            pltpu.VMEM((groups, per, LANES), BF16),
+            pltpu.SemaphoreType.DMA((2,)),
+            pltpu.SemaphoreType.DMA((2,)),
+            pltpu.SemaphoreType.DMA((2,)),
         ],
-        compiler_params=pltpu.CompilerParams(vmem_limit_bytes=48 << 20),
+        compiler_params=pltpu.CompilerParams(vmem_limit_bytes=40 << 20, collective_id=0, has_side_effects=True),
         name="high",
     )(hi_ainv, record, hi_send, lift_ref, trace_hi, face_mass, placed)
-
-    arrived = lax.all_to_all(outgoing, "geo", split_axis=0, concat_axis=0, tiled=True)
 
     plan = recv_face.reshape(groups, 2 * capacity)
     share = width // 7
@@ -351,6 +443,7 @@
         grid=(tiles + 7,),
         in_specs=[
             pl.BlockSpec((groups, per, LANES), lambda q: (0, 0, 0)),
+            pl.BlockSpec((groups, LOW_ROWS, LANES), lambda q: (0, 0, 0)),
             pl.BlockSpec((groups, 2 * capacity), lambda q: (0, 0)),
         ],
         out_specs=(
@@ -359,6 +452,7 @@
         ),
         scratch_shapes=[
             pltpu.VMEM((groups * (per + SKEW), LANES), F32),
+            pltpu.VMEM((groups * (LOW_ROWS + SKEW), LANES), F32),
             pltpu.VMEM((groups * capacity, faces), BF16),
             pltpu.VMEM((groups * capacity, faces), BF16),
             pltpu.VMEM((LANES, faces), F32),
@@ -366,7 +460,7 @@
         ],
         compiler_params=pltpu.CompilerParams(vmem_limit_bytes=48 << 20),
         name="accumulate",
-    )(arrived, plan)
+    )(arrived, low_arrived, plan)
     return (low_particular, high_particular, blocks, right)
 
 

time: 95.9 us -> 89.1 us (0.929)
  Pallas kernels: 24.7 us -> 76.1 us
  waiting for transfers between devices: 41 us -> 0.01 us
  starting transfers between devices: 22.8 us -> 4.84 us
  local copies, waits for them, and re-layouts: 4.72 us -> 5.99 us
    pallas_call x1, Pallas kernels: 12.2 us -> 63.3 us  [on_device(): pl.pallas_call(functools.partial(high_kernel, capacity), out_shape=(jax.S...]
    all_to_all x1 -> x0, waiting for transfers between devices: 41 us -> none  [on_device(): lax.all_to_all(outgoing, 'geo', split_axis=0, concat_axis=0, tiled=True)]
    all_to_all x1 -> x0, starting transfers between devices: 18 us -> none  [on_device(): lax.all_to_all(outgoing, 'geo', split_axis=0, concat_axis=0, tiled=True)]
    unnamed x13 -> x12, local copies, waits for them, and re-layouts: 3.63 us -> 4.2 us
  transfers between devices with their start and end apart: 2 -> 1, of which waited for: 1 -> 0; matrix products, arithmetic and copies ran while one was open for 4% -> 5% of each run, Pallas kernels for 4% -> 5%
where the time goes in v3:
time: 89.1 us; the launch traced here: 88.7 us
  Pallas kernels  76.1 us (85%)
  local copies, waits for them, and re-layouts  5.99 us (7%)
  starting transfers between devices  4.84 us (5%)
  other arithmetic  0.98 us (1%)
    pallas_call x1, Pallas kernels, on_device(): pl.pallas_call(functools.partial(high_kernel, capacity), out_shape=(jax.S...  63.3 us
    pallas_call x1, Pallas kernels, on_device(): pl.pallas_call(functools.partial(accumulate_kernel, capacity, width), out...  6.9 us
    all_to_all x1, starting transfers between devices, on_device(): lax.all_to_all(record, 'deg', split_axis=0, concat_axis=0, tiled=True)  4.84 us
    unnamed x12, local copies, waits for them, and re-layouts  4.2 us
    pallas_call x1, Pallas kernels, on_device(): pl.pallas_call(functools.partial(low_kernel, capacity), out_shape=(jax.Sh...  4.16 us
  transfers between devices with their start and end apart: 1, of which 0 were waited for; matrix products, arithmetic and copies ran while one was open for 5% of the time, Pallas kernels for 5%

profile of v3, /device:TPU:1, one launch (start us, length us, event | category | flops | bytes accessed | tf_op | source)
XLA Modules:
  0.0 88.7 jit_solution(16376122328686037139)
XLA Ops:
  0.6 0.0 copy-start.3
  0.6 0.0 copy-start.4
  0.7 0.0 copy-start
  0.7 1.7 %record.1 = f32[128,128]{1,0:T(8,128)} custom-call(f32[12,128]{1,0:T(8,128)} %geom_ref.3, bf16[84,128]{1,0:T(8,128)(2,1)} %load_ref.3, s32[1,128]{1,0:T(1,128)} %bitcast.13, s32[1,128]{1,0:T(1,128)} %bitcast.14), custom_call_target="tpu_custom_call" | custom-call | tf_op jit(solution)/shard_map/record/pallas_call | solution.py:364
  2.4 4.8 %all-to-all-start = ((f32[4,32,128]{2,1,0:T(8,128)}), f32[4,32,128]{2,1,0:T(8,128)S(1)}, u32[]{:S(2)}, u32[]{:S(2)}) async-start(f32[4,32,128]{2,1,0:T(8,128)} %bitcast.12), calls=%async_computation | async-start | bytes 131072 | tf_op jit(solution)/shard_map/all_to_all | solution.py:371
  7.2 1.0 %convert_bitcast_fusion = bf16[4,4,28,84]{3,1,2,0:T(4,128)(2,1)S(1)} fusion(f32[4,84,4,28]{1,2,3,0:T(4,128)} %param.28), kind=kLoop, calls=%fused_computation | loop fusion | flops 37632 | bytes 225792 | tf_op jit(solution)/shard_map/convert.4
  8.2 0.1 pad_bitcast_fusion
  8.4 0.8 reshape.17.recv_ref
  9.2 0.1 convert_element_type.17.trace_ref
  9.4 0.7 convert_element_type.15.trace_ref
  10.1 1.7 %copy.24.lift_ref = f32[4,4,28,84]{3,2,1,0:T(8,128)} copy(f32[4,4,28,84]{3,1,2,0:T(4,128)} %param.27) | data formatting | bytes 301056 | tf_op args[12]
  11.7 4.2 %low.1 = (f32[20,128]{1,0:T(8,128)}, bf16[128,8,128]{2,1,0:T(8,128)(2,1)}) custom-call(bf16[20,20,128]{2,1,0:T(8,128)(2,1)} %ainv_ref.2, f32[12,128]{1,0:T(8,128)} %geom_ref.2, bf16[20,128]{1,0:T(8,128)(2,1)} %load_ref.2, s32[1,128]{1,0:T(1,128)} %bitcast.15, s32[4,128]{1,0:T(4,128)} %send_ref.2, f32[4,4,28,84]{3,2,1,0:T(8,128)} %copy.24.lift_ref, ...), custom_call_target="tpu_custom_call" | custom-call | flops 400000000 | bytes 2000000 | tf_op jit(solution)/shard_map/low/pallas_call | solution.py:383
  15.9 0.0 all-to-all-done
  15.9 0.0 copy-done.3
  15.9 0.0 copy-done.4
  15.9 0.0 copy-done
  15.9 0.0 copy-start.1
  15.9 0.9 %copy-done.1 = f32[4,4,28,84]{3,2,1,0:T(8,128)S(1)} copy-done((f32[4,4,28,84]{3,2,1,0:T(8,128)S(1)}, f32[4,4,28,84]{3,2,1,0:T(8,128)}, u32[]{:S(2)}) %copy-start.1) | copy-done | bytes 150552
  16.9 0.0 copy-start.2
  16.9 0.9 %copy-done.2 = bf16[128,8,128]{2,1,0:T(8,128)(2,1)S(1)} copy-done((bf16[128,8,128]{2,1,0:T(8,128)(2,1)S(1)}, bf16[128,8,128]{2,1,0:T(8,128)(2,1)}, u32[]{:S(2)}) %copy-start.2) | copy-done | bytes 262168
  17.8 63.3 %high.1 = (f32[84,128]{1,0:T(8,128)S(1)}, bf16[128,40,128]{2,1,0:T(8,128)(2,1)S(1)}, bf16[128,8,128]{2,1,0:T(8,128)(2,1)S(1)}) custom-call(bf16[84,84,128]{2,1,0:T(8,128)(2,1)S(1)} %copy-done, f32[128,128]{1,0:T(8,128)S(1)} %bitcast.11, s32[4,128]{1,0:T(4,128)S(1)} %copy-done.4, f32[4,4,28,84]{3,2,1,0:T(8,128)S(1)} %copy-done.1, ...), custom_call_target="tpu_custom_call" | custom-call | tf_op jit(solution)/shard_map/high/pallas_call | solution.py:406
  81.1 6.9 %accumulate.1 = (f32[28,28,768]{2,1,0:T(8,128)}, f32[28,768]{1,0:T(8,128)}) custom-call(bf16[128,40,128]{2,1,0:T(8,128)(2,1)S(1)} %get-tuple-element.14.rows_ref, bf16[128,8,128]{2,1,0:T(8,128)(2,1)S(1)} %get-tuple-element.15.low_ref, s32[128,12]{1,0:T(8,128)S(1)} %reshape.17.recv_ref), custom_call_target="tpu_custom_call" | custom-call | tf_op jit(solution)/shard_map/accumulate/pallas_call | solution.py:437
  88.0 0.6 copy.28
  (4 shorter events, 0.1 us)
Async XLA Ops:
  0.6 15.3 %copy-start.3 = (f32[28,28]{1,0:T(8,128)S(1)}, f32[28,28]{1,0:T(8,128)}, u32[]{:S(2)}) copy-start(f32[28,28]{1,0:T(8,128)} %mass_ref.3) | copy-start | bytes 9412
  0.6 15.3 %copy-start.4 = (s32[4,128]{1,0:T(4,128)S(1)}, s32[4,128]{1,0:T(4,128)}, u32[]{:S(2)}) copy-start(s32[4,128]{1,0:T(4,128)} %send_ref.3) | copy-start | bytes 6148
  0.7 15.3 %copy-start = (bf16[84,84,128]{2,1,0:T(8,128)(2,1)S(1)}, bf16[84,84,128]{2,1,0:T(8,128)(2,1)}, u32[]{:S(2)}) copy-start(bf16[84,84,128]{2,1,0:T(8,128)(2,1)} %ainv_ref.3) | copy-start | bytes 5419012
  2.4 13.5 %all-to-all-start = ((f32[4,32,128]{2,1,0:T(8,128)}), f32[4,32,128]{2,1,0:T(8,128)S(1)}, u32[]{:S(2)}, u32[]{:S(2)}) async-start(f32[4,32,128]{2,1,0:T(8,128)} %bitcast.12), calls=%async_computation | async-start | bytes 131072 | tf_op jit(solution)/shard_map/all_to_all | solution.py:371
  15.9 1.0 %copy-start.1 = (f32[4,4,28,84]{3,2,1,0:T(8,128)S(1)}, f32[4,4,28,84]{3,2,1,0:T(8,128)}, u32[]{:S(2)}) copy-start(f32[4,4,28,84]{3,2,1,0:T(8,128)} %copy.24.lift_ref) | copy-start | bytes 451588
  16.9 0.9 %copy-start.2 = (bf16[128,8,128]{2,1,0:T(8,128)(2,1)S(1)}, bf16[128,8,128]{2,1,0:T(8,128)(2,1)}, u32[]{:S(2)}) copy-start(bf16[128,8,128]{2,1,0:T(8,128)(2,1)} %get-tuple-element.12.low_ref) | copy-start | bytes 786436
